TPU v7x, 128 devices: a whole 4x4x4 slice. The times are simulated.
128 devices in a mesh: segment: 2 (over z_lo), expert: 32 (over x, y, core), dp: 2 (over z_hi).
Axes of the slice: x: 4, y: 4, z: 4 (z_hi: 2, z_lo: 2; z = z_hi * 2 + z_lo), core: 2. Of those that a mesh axis runs over, the one named last changes fastest.
Arguments:
- features: bfloat16 [2, 4096, 512], P(None, ('expert', 'dp')), may hold values from -6 to 6
- routes: int32 [2, 4096, 2], P(None, ('expert', 'dp')), may hold values from 0 to 31, all different within a row; in each aligned block of 64 rows (0 to 63, 64 to 127, ..., all dimensions but the last counted through in order) at most 8 rows name the same one
- arm_ids: int32 [2, 4096], P(None, ('expert', 'dp')), may hold values from 0 to 5
- targets: float32 [2, 4096], P(None, ('expert', 'dp')), may hold values from -6 to 6
- trunk_gain: float32 [512], replicated, may hold values from 0.5 to 1.5
- gate_weight: bfloat16 [32, 512, 4096], P('expert', None, ('segment', 'dp')), may hold values from -0.25 to 0.25
- up_weight: bfloat16 [32, 512, 4096], P('expert', None, ('segment', 'dp')), may hold values from -0.25 to 0.25
- down_weight: bfloat16 [32, 4096, 512], P('expert', ('segment', 'dp')), may hold values from -0.09375 to 0.09375
- tower_in: bfloat16 [7, 512, 8192], P(None, None, ('segment', 'expert', 'dp')), may hold values from -0.25 to 0.25
- tower_out: bfloat16 [7, 8192], P(None, ('segment', 'expert', 'dp')), may hold values from -0.0625 to 0.0625
Outputs:
- grad_gate: bfloat16 [32, 512, 4096], P('expert', None, ('segment', 'dp'))
- grad_up: bfloat16 [32, 512, 4096], P('expert', None, ('segment', 'dp'))
- grad_down: bfloat16 [32, 4096, 512], P('expert', ('segment', 'dp'))
- grad_tower_in: bfloat16 [7, 512, 8192], P(None, None, ('segment', 'expert', 'dp'))
- grad_tower_out: bfloat16 [7, 8192], P(None, ('segment', 'expert', 'dp'))
- grad_gain: float32 [512], replicated
Inputs may be any that keep to these rules, and one draw needn't show every extreme that they name: `routes`: each row names 2 different experts; within every micro-batch, each aligned block of 64 rows names any one expert at most 8 times, a bound that some block reaches.
All inputs are finite; a program needn't handle non-finite values.
Results may differ from a plain program's by a relative error of at most 0.023.
Values may be sent and summed in bfloat16 or wider, within the bound.
A program may use at most 256 MiB of HBM per device.

v0:
```python
import jax
import jax.numpy as jnp
from jax import lax
from jax.sharding import PartitionSpec as P

EPSILON = 1e-06


def shifted(value, axis, steps):
    count = lax.axis_size(axis)
    leading, last = (max(0, -steps), min(count, count - steps))
    return lax.ppermute(value, axis, [(source, source + steps) for source in range(leading, last)])


def silu_slope(value):
    sig_value = jax.nn.sigmoid(value)
    return sig_value * (1.0 + value * (1.0 - sig_value))


def norm_rows(features, trunk_gain):
    wide_rows = features.astype(jnp.float32)
    scaled = wide_rows * lax.rsqrt(
        jnp.mean(wide_rows * wide_rows, axis=-1, keepdims=True) + EPSILON
    )
    return (scaled, (scaled * trunk_gain).astype(jnp.bfloat16))


def slot_matrix(routes, experts, capacity):
    row_count, top_count = routes.shape
    flat_ids = routes.reshape(row_count * top_count)
    onehot = (flat_ids[:, None] == jnp.arange(experts, dtype=jnp.int32)[None, :]).astype(jnp.int32)
    before = jnp.cumsum(onehot, axis=0) - onehot
    slot_rank = jnp.sum(before * onehot, axis=1)
    position = flat_ids * capacity + slot_rank
    columns = jnp.arange(experts * capacity, dtype=jnp.int32)[None, :]
    slot_table = (position[:, None] == columns).astype(jnp.bfloat16)
    return jnp.sum(slot_table.reshape(row_count, top_count, experts * capacity), axis=1)


def expert_forward(received, w_gate, w_up):
    local_count = w_gate.shape[0]
    slot_total, slot_count, feature_width = received.shape
    grouped = received.reshape(slot_total // local_count, local_count, slot_count, feature_width)
    gate_pre = jnp.einsum("sekd,edf->sekf", grouped, w_gate, preferred_element_type=jnp.float32)
    up_pre = jnp.einsum("sekd,edf->sekf", grouped, w_up, preferred_element_type=jnp.float32)
    active = (jax.nn.silu(gate_pre) * up_pre).astype(jnp.bfloat16)
    return (grouped, gate_pre, up_pre, active)


def trunk_forward(features, routes, trunk_gain, trunk_weights, capacity):
    w_gate, w_up, w_down = trunk_weights
    experts = w_gate.shape[0] * lax.axis_size("expert")
    feature_width = features.shape[1]
    scaled, normed = norm_rows(features, trunk_gain)
    slot_table = slot_matrix(routes, experts, capacity)
    outgoing = jnp.dot(slot_table.T, normed, preferred_element_type=jnp.float32).astype(
        jnp.bfloat16
    )
    outgoing = outgoing.reshape(experts, capacity, feature_width)
    received = lax.all_to_all(outgoing, "expert", split_axis=0, concat_axis=0, tiled=True)
    grouped, gate_pre, up_pre, active = expert_forward(received, w_gate, w_up)
    produced = jnp.einsum("sekf,efd->sekd", active, w_down, preferred_element_type=jnp.float32)
    produced = produced.astype(jnp.bfloat16).reshape(received.shape)
    returned = lax.all_to_all(produced, "expert", split_axis=0, concat_axis=0, tiled=True)
    returned, received = (returned, received)
    added = jnp.dot(
        slot_table,
        returned.reshape(experts * capacity, feature_width),
        preferred_element_type=jnp.float32,
    )
    mixed_rows = (features.astype(jnp.float32) + added).astype(jnp.bfloat16)
    return (mixed_rows, (slot_table, received, scaled))


def trunk_backward(grad_mixed, saved_state, trunk_weights, trunk_sums):
    w_gate, w_up, w_down = trunk_weights
    slot_table, received, scaled = saved_state
    experts, capacity, feature_width = received.shape
    outgoing = jnp.dot(slot_table.T, grad_mixed, preferred_element_type=jnp.float32).astype(
        jnp.bfloat16
    )
    arrived = lax.all_to_all(
        outgoing.reshape(experts, capacity, feature_width),
        "expert",
        split_axis=0,
        concat_axis=0,
        tiled=True,
    )
    grouped, gate_pre, up_pre, active = expert_forward(received, w_gate, w_up)
    grad_out = arrived.reshape(grouped.shape)
    grad_active = jnp.einsum("sekd,efd->sekf", grad_out, w_down, preferred_element_type=jnp.float32)
    grad_gate_pre = (grad_active * up_pre * silu_slope(gate_pre)).astype(jnp.bfloat16)
    grad_up_pre = (grad_active * jax.nn.silu(gate_pre)).astype(jnp.bfloat16)
    sum_gate, sum_up, sum_down, sum_gain = trunk_sums
    sum_gate = sum_gate + jnp.einsum(
        "sekd,sekf->edf", grouped, grad_gate_pre, preferred_element_type=jnp.float32
    )
    sum_up = sum_up + jnp.einsum(
        "sekd,sekf->edf", grouped, grad_up_pre, preferred_element_type=jnp.float32
    )
    sum_down = sum_down + jnp.einsum(
        "sekf,sekd->efd", active, grad_out, preferred_element_type=jnp.float32
    )
    grad_part = jnp.einsum(
        "sekf,edf->sekd", grad_gate_pre, w_gate, preferred_element_type=jnp.float32
    )
    grad_part = grad_part + jnp.einsum(
        "sekf,edf->sekd", grad_up_pre, w_up, preferred_element_type=jnp.float32
    )
    grad_part = grad_part.astype(jnp.bfloat16).reshape(experts, capacity, feature_width)
    back_slots = lax.all_to_all(grad_part, "expert", split_axis=0, concat_axis=0, tiled=True)
    grad_rows = jnp.dot(
        slot_table,
        back_slots.reshape(experts * capacity, feature_width),
        preferred_element_type=jnp.float32,
    )
    sum_gain = sum_gain + jnp.sum(grad_rows * scaled, axis=0)
    return (sum_gate, sum_up, sum_down, sum_gain)


def loss_grad(tower_value, arm_ids, targets, loss_scale):
    treated = (arm_ids != 0).astype(jnp.float32)
    propensity = loss_scale * (jax.nn.sigmoid(tower_value[:, 0]) - treated)
    arm_range = jnp.arange(tower_value.shape[1] - 1, dtype=jnp.int32)[None, :]
    picked_arm = (arm_ids[:, None] == arm_range).astype(jnp.float32)
    outcome = loss_scale * (tower_value[:, 1:] - targets[:, None]) * picked_arm
    return jnp.concatenate([propensity[:, None], outcome], axis=1)


def tower_step(arrived, arm_ids, targets, tower_weights, tower_sums, loss_scale):
    w_in, w_out = tower_weights
    row_piece = lax.all_gather(arrived, "expert", axis=0, tiled=True)
    pre_act = jnp.einsum("rd,tdj->rtj", row_piece, w_in, preferred_element_type=jnp.float32)
    hidden = jax.nn.silu(pre_act).astype(jnp.bfloat16)
    partial_value = jnp.einsum("rtj,tj->rt", hidden, w_out, preferred_element_type=jnp.float32)
    gathered, pre_act, partial_value = (row_piece, pre_act, partial_value)
    tower_value = lax.psum_scatter(
        partial_value.astype(jnp.bfloat16), "expert", scatter_dimension=0, tiled=True
    ).astype(jnp.float32)
    grad_own = loss_grad(tower_value, arm_ids, targets, loss_scale)
    grad_value = lax.all_gather(grad_own, "expert", axis=0, tiled=True)
    grad_pre = (
        grad_value[:, :, None] * w_out.astype(jnp.float32)[None] * silu_slope(pre_act)
    ).astype(jnp.bfloat16)
    hidden = jax.nn.silu(pre_act).astype(jnp.bfloat16)
    sum_in, sum_out = tower_sums
    sum_in = sum_in + jnp.einsum(
        "rd,rtj->tdj", gathered, grad_pre, preferred_element_type=jnp.float32
    )
    sum_out = sum_out + jnp.einsum(
        "rt,rtj->tj", grad_value.astype(jnp.bfloat16), hidden, preferred_element_type=jnp.float32
    )
    grad_rows = lax.psum_scatter(
        jnp.einsum("rtj,tdj->rd", grad_pre, w_in, preferred_element_type=jnp.float32).astype(
            jnp.bfloat16
        ),
        "expert",
        scatter_dimension=0,
        tiled=True,
    )
    return (grad_rows, (sum_in, sum_out))


def move_up(rows_sent):
    return shifted(rows_sent, "segment", 1)


def move_down(rows_sent):
    return shifted(rows_sent, "segment", -1)


def body(
    features,
    routes,
    arm_ids,
    targets,
    trunk_gain,
    gate_weight,
    up_weight,
    down_weight,
    tower_in,
    tower_out,
):
    batches, rows_here, feature_width = features.shape
    experts = gate_weight.shape[0] * lax.axis_size("expert")
    capacity = max(2, 2 * routes.shape[2] * rows_here // experts)
    loss_scale = float(batches * rows_here * lax.axis_size("expert") * lax.axis_size("dp")) ** (
        -0.5
    )
    is_trunk = lax.axis_index("segment") == 0
    gathered = (
        lax.all_gather(gate_weight, ("segment", "dp"), axis=2, tiled=True),
        lax.all_gather(up_weight, ("segment", "dp"), axis=2, tiled=True),
        lax.all_gather(down_weight, ("segment", "dp"), axis=1, tiled=True),
        lax.all_gather(tower_in, ("segment", "dp"), axis=2, tiled=True),
        lax.all_gather(tower_out, ("segment", "dp"), axis=1, tiled=True),
    )
    trunk_weights = (gathered[0], gathered[1], gathered[2])
    tower_weights = (gathered[3], gathered[4])
    blank_rows = jnp.zeros((rows_here, feature_width), jnp.bfloat16)
    blank_state = (
        jnp.zeros((rows_here, experts * capacity), jnp.bfloat16),
        jnp.zeros((experts, capacity, feature_width), jnp.bfloat16),
        jnp.zeros((rows_here, feature_width), jnp.float32),
    )
    trunk_sums = (
        jnp.zeros(gathered[0].shape, jnp.float32),
        jnp.zeros(gathered[1].shape, jnp.float32),
        jnp.zeros(gathered[2].shape, jnp.float32),
        jnp.zeros((feature_width,), jnp.float32),
    )
    tower_sums = (
        jnp.zeros(gathered[3].shape, jnp.float32),
        jnp.zeros(gathered[4].shape, jnp.float32),
    )
    saved_list = [blank_state] * batches

    def select_section(trunk_side, tower_side):
        return jax.tree.map(
            lambda first, second: jnp.where(is_trunk, first, second), trunk_side, tower_side
        )

    def run_tick(forward_at, tower_at, backward_at, from_below, from_above, trunk_sums, tower_sums):
        sent_up = blank_rows
        saved_state = blank_state
        new_trunk = trunk_sums
        if forward_at is not None:
            sent_up, saved_state = trunk_forward(
                features[forward_at], routes[forward_at], trunk_gain, trunk_weights, capacity
            )
        if backward_at is not None:
            new_trunk = trunk_backward(
                from_above, saved_list[backward_at], trunk_weights, trunk_sums
            )
        sent_down = blank_rows
        new_tower = tower_sums
        if tower_at is not None:
            sent_down, new_tower = tower_step(
                from_below,
                arm_ids[tower_at],
                targets[tower_at],
                tower_weights,
                tower_sums,
                loss_scale,
            )
        return (
            select_section(sent_up, blank_rows),
            select_section(blank_rows, sent_down),
            saved_state,
            select_section(new_trunk, trunk_sums),
            select_section(tower_sums, new_tower),
        )

    from_below = blank_rows
    from_above = blank_rows
    arrived_grads = [blank_rows] * batches
    for step_index in range(batches + 1):
        forward_at = step_index if step_index < batches else None
        tower_at = step_index - 1 if step_index >= 1 else None
        sent_up, sent_down, saved_state, trunk_sums, tower_sums = run_tick(
            forward_at, tower_at, None, from_below, blank_rows, trunk_sums, tower_sums
        )
        if forward_at is not None:
            saved_list[forward_at] = saved_state
            from_below = move_up(sent_up)
        if tower_at is not None:
            arrived_grads[tower_at] = move_down(sent_down)
    for backward_at in reversed(range(batches)):
        outcome_state = run_tick(
            None, None, backward_at, blank_rows, arrived_grads[backward_at], trunk_sums, tower_sums
        )
        trunk_sums = outcome_state[3]
        tower_sums = outcome_state[4]
    grad_gain = lax.psum(trunk_sums[3], ("segment", "expert", "dp"))
    reduced = (
        lax.psum_scatter(
            trunk_sums[0].astype(jnp.bfloat16), ("segment", "dp"), scatter_dimension=2, tiled=True
        ).astype(jnp.float32),
        lax.psum_scatter(
            trunk_sums[1].astype(jnp.bfloat16), ("segment", "dp"), scatter_dimension=2, tiled=True
        ).astype(jnp.float32),
        lax.psum_scatter(
            trunk_sums[2].astype(jnp.bfloat16), ("segment", "dp"), scatter_dimension=1, tiled=True
        ).astype(jnp.float32),
        lax.psum_scatter(
            tower_sums[0].astype(jnp.bfloat16), ("segment", "dp"), scatter_dimension=2, tiled=True
        ).astype(jnp.float32),
        lax.psum_scatter(
            tower_sums[1].astype(jnp.bfloat16), ("segment", "dp"), scatter_dimension=1, tiled=True
        ).astype(jnp.float32),
    )
    return (
        reduced[0].astype(jnp.bfloat16),
        reduced[1].astype(jnp.bfloat16),
        reduced[2].astype(jnp.bfloat16),
        reduced[3].astype(jnp.bfloat16),
        reduced[4].astype(jnp.bfloat16),
        grad_gain,
    )


def solution(mesh):
    in_specs = (
        P(None, ("expert", "dp"), None),
        P(None, ("expert", "dp"), None),
        P(None, ("expert", "dp")),
        P(None, ("expert", "dp")),
        P(),
        P("expert", None, ("segment", "dp")),
        P("expert", None, ("segment", "dp")),
        P("expert", ("segment", "dp"), None),
        P(None, None, ("segment", "expert", "dp")),
        P(None, ("segment", "expert", "dp")),
    )
    out_specs = (
        P("expert", None, ("segment", "dp")),
        P("expert", None, ("segment", "dp")),
        P("expert", ("segment", "dp"), None),
        P(None, None, ("segment", "expert", "dp")),
        P(None, ("segment", "expert", "dp")),
        P(),
    )
    return jax.shard_map(body, mesh=mesh, in_specs=in_specs, out_specs=out_specs, check_vma=False)
```

profile of v0, /device:TPU:1, one launch (start us, length us, event | category | flops | bytes accessed | tf_op | source)
XLA Modules:
  0.0 1113.0 jit_solution(4312872654614399548)
XLA Ops:
  15.6 8.6 all-to-all-start.3
  24.8 8.4 all-to-all-done.3
  33.1 61.7 %all-gather.12.cloned.1.call-done = bf16[1,512,4096]{2,1,0:T(8,128)(2,1)} async-done(((bf16[1,512,1024]{2,1,0:T(8,128)(2,1)}), bf16[1,512,4096]{2,1,0:T(8,128)(2,1)}) %all-gather.12.cloned.1.call-update) | async-done | bytes 4194320 | tf_op jit(solution)/shard_map/all_gather | solution.py:193
  100.3 77.4 %all-gather.10.cloned.1.call-done = bf16[1,512,4096]{2,1,0:T(8,128)(2,1)} async-done(((bf16[1,512,1024]{2,1,0:T(8,128)(2,1)}), bf16[1,512,4096]{2,1,0:T(8,128)(2,1)}) %all-gather.10.cloned.1.call-update) | async-done | bytes 4194320 | tf_op jit(solution)/shard_map/all_gather | solution.py:192
  184.6 76.0 %all-gather.14.cloned.1.call-done = bf16[1,4096,512]{2,1,0:T(8,128)(2,1)} async-done(((bf16[1,1024,512]{2,1,0:T(8,128)(2,1)}), bf16[1,4096,512]{2,1,0:T(8,128)(2,1)}) %all-gather.14.cloned.1.call-update) | async-done | bytes 4194320 | tf_op jit(solution)/shard_map/all_gather | solution.py:194
  272.5 8.9 all-to-all-done.4
  286.9 13.3 %all_to_all.40 = bf16[32,8,512]{2,1,0:T(8,128)(2,1)S(1)} all-to-all(bf16[32,8,512]{2,1,0:T(8,128)(2,1)S(1)} %fusion.72), channel_id=1, replica_groups=mesh['segment'=2,'expert'=32,'dp'=2] {'expert'}, dimensions={0} | all-to-all | bytes 524288 | tf_op jit(solution)/shard_map/all_to_all | solution.py:60
  316.2 11.3 %all-gather = bf16[4,64,7]{1,2,0:T(8,128)(2,1)S(1)} all-gather(bf16[1,64,7]{1,2,0:T(8,128)(2,1)S(1)} %bitcast.329), channel_id=1, replica_groups=mesh['segment'=2,'expert'=32,'dp'=2] {'segment','dp'}, dimensions={0}, use_global_device_ids=true | all-gather | bytes 4480 | tf_op jit(solution)/shard_map/all_gather | solution.py:196
  332.3 19.7 %all-gather.20.cloned.1.call-done = bf16[2048,512]{1,0:T(8,128)(2,1)} async-done(((bf16[64,512]{1,0:T(8,128)(2,1)}), bf16[2048,512]{1,0:T(8,128)(2,1)}) %all-gather.20.cloned.1.call-update) | async-done | bytes 2097168 | tf_op jit(solution)/shard_map/all_gather | solution.py:132
  352.0 10.2 multiply_convert_fusion.1
  368.5 29.0 %all-gather.16.cloned.1.call-done = bf16[2048,512]{1,0:T(8,128)(2,1)} async-done(((bf16[64,512]{1,0:T(8,128)(2,1)}), bf16[2048,512]{1,0:T(8,128)(2,1)}) %all-gather.16.cloned.1.call-update) | async-done | bytes 2097168 | tf_op jit(solution)/shard_map/all_gather | solution.py:132
  397.5 11.1 multiply_convert_fusion.3
  414.8 61.3 %reduce-scatter.30.cloned.1.call-done = bf16[64,7]{1,0:T(8,128)(2,1)} async-done(((bf16[2048,7]{1,0:T(8,128)(2,1)}), bf16[64,7]{1,0:T(8,128)(2,1)}) %reduce-scatter.30.cloned.1.call-update) | async-done | bytes 912
  476.9 79.8 %reduce-scatter.28.cloned.1.call-done = bf16[64,7]{1,0:T(8,128)(2,1)} async-done(((bf16[2048,7]{1,0:T(8,128)(2,1)}), bf16[64,7]{1,0:T(8,128)(2,1)}) %reduce-scatter.28.cloned.1.call-update) | async-done | bytes 912
  557.6 26.4 %all-gather.1 = f32[32,64,7]{1,2,0:T(8,128)S(1)} all-gather(f32[1,64,7]{1,2,0:T(8,128)S(1)} %maximum_bitcast_fusion), channel_id=1, replica_groups=mesh['segment'=2,'expert'=32,'dp'=2] {'expert'}, dimensions={0}, use_global_device_ids=true | all-gather | bytes 59136 | tf_op jit(solution)/shard_map/all_gather | solution.py:141
  584.0 22.5 %all-gather.2 = f32[32,64,7]{1,2,0:T(8,128)S(1)} all-gather(f32[1,64,7]{1,2,0:T(8,128)S(1)} %maximum_bitcast_fusion.1), channel_id=1, replica_groups=mesh['segment'=2,'expert'=32,'dp'=2] {'expert'}, dimensions={0}, use_global_device_ids=true | all-gather | bytes 59136 | tf_op jit(solution)/shard_map/all_gather | solution.py:141
  606.7 13.4 %multiply_convert_fusion = (bf16[2048,7,256]{2,0,1:T(8,128)(2,1)}, bf16[2048,7,256]{2,0,1:T(8,128)(2,1)S(1)}) fusion(f32[2048,7,256]{2,0,1:T(8,128)} %get-tuple-element.25, f32[2048,7]{0,1:T(8,128)S(1)} %reshape.281, f32[7,256]{1,0:T(8,128)S(1)} %bitcast_convert_fusion.4, f32[2048,7,256]{2,0,1:T(8,128)} %get-tuple-element.27, f32[2048,7]{0,1:T(8,128)S(1)} %reshape.279), kind=kLoop, calls=%fused_computation | loop fusion | flops 73400320 | bytes 44162048 | tf_op jit(solution)/shard_map/convert_element_type | solution.py:144
  646.0 9.7 fusion.33
  655.7 48.2 %reduce-scatter.16.cloned.1.call-done = bf16[64,512]{1,0:T(8,128)(2,1)} async-done(((bf16[2048,512]{1,0:T(8,128)(2,1)}), bf16[64,512]{1,0:T(8,128)(2,1)}) %reduce-scatter.16.cloned.1.call-update) | async-done | bytes 65552 | tf_op jit(solution)/shard_map/reduce_scatter | solution.py:153
  705.3 80.3 %reduce-scatter.18.cloned.1.call-done = bf16[64,512]{1,0:T(8,128)(2,1)} async-done(((bf16[2048,512]{1,0:T(8,128)(2,1)}), bf16[64,512]{1,0:T(8,128)(2,1)}) %reduce-scatter.18.cloned.1.call-update) | async-done | bytes 65552 | tf_op jit(solution)/shard_map/reduce_scatter | solution.py:153
  795.2 9.0 fusion.26
  890.2 96.5 %psum.7 = f32[512]{0:T(512)} all-reduce(f32[512]{0:T(512)S(1)} %add_select_fusion.5), channel_id=1, replica_groups=mesh['segment'=2,'expert'=32,'dp'=2] {'segment','expert','dp'}, use_global_device_ids=true, to_apply=%region_19.20 | all-reduce | flops 512 | bytes 4096 | tf_op jit(solution)/shard_map/psum | solution.py:274
  986.7 37.0 %reduce-scatter.20.cloned.1.call-done = bf16[1,512,1024]{2,1,0:T(8,128)(2,1)} async-done(((bf16[1,512,4096]{2,1,0:T(8,128)(2,1)}), bf16[1,512,1024]{2,1,0:T(8,128)(2,1)}) %reduce-scatter.20.cloned.1.call-update) | async-done | bytes 1048592 | tf_op jit(solution)/shard_map/reduce_scatter | solution.py:276
  1023.7 82.6 %reduce-scatter.22.cloned.1.call-done = bf16[1,512,1024]{2,1,0:T(8,128)(2,1)} async-done(((bf16[1,512,4096]{2,1,0:T(8,128)(2,1)}), bf16[1,512,1024]{2,1,0:T(8,128)(2,1)}) %reduce-scatter.22.cloned.1.call-update) | async-done | bytes 1048592 | tf_op jit(solution)/shard_map/reduce_scatter | solution.py:279
  (227 shorter events, 196.0 us)
Async XLA Ops:
  7.2 87.7 %all-gather.12.cloned.1.call-start = ((), (), s32[]{:S(2)}) async-start(), calls=%async_computation.18 | async-start | bytes 5242880 | tf_op jit(solution)/shard_map/all_gather | solution.py:193
  7.9 169.8 %all-gather.10.cloned.1.call-start = ((), (), s32[]{:S(2)}) async-start(), calls=%async_computation.17 | async-start | bytes 5242880 | tf_op jit(solution)/shard_map/all_gather | solution.py:192
  8.6 251.9 %all-gather.14.cloned.1.call-start = ((), (), s32[]{:S(2)}) async-start(), calls=%async_computation.19 | async-start | bytes 5242880 | tf_op jit(solution)/shard_map/all_gather | solution.py:194
  15.6 17.5 %all-to-all-start.3 = ((bf16[32,8,512]{2,1,0:T(8,128)(2,1)}), bf16[32,8,512]{2,1,0:T(8,128)(2,1)S(1)}, u32[]{:S(2)}, u32[]{:S(2)}) async-start(bf16[32,8,512]{2,1,0:T(8,128)(2,1)} %fusion.74), calls=%async_computation.4 | async-start | bytes 524288 | tf_op jit(solution)/shard_map/all_to_all | solution.py:60
  24.2 308.1 %all-gather.18.cloned.1.call-start = ((), (), s32[]{:S(2)}) async-start(), calls=%async_computation.21 | async-start | bytes 2293760 | tf_op jit(solution)/shard_map/all_gather | solution.py:195
  264.7 16.7 %all-to-all-start.4 = ((bf16[32,8,512]{2,1,0:T(8,128)(2,1)}), bf16[32,8,512]{2,1,0:T(8,128)(2,1)S(1)}, u32[]{:S(2)}, u32[]{:S(2)}) async-start(bf16[32,8,512]{2,1,0:T(8,128)(2,1)} %fusion.69), calls=%async_computation.5 | async-start | bytes 524288 | tf_op jit(solution)/shard_map/all_to_all | solution.py:64
  272.4 79.6 %all-gather.20.cloned.1.call-start = ((), (), s32[]{:S(2)}) async-start(), calls=%async_computation.23 | async-start | bytes 2162688 | tf_op jit(solution)/shard_map/all_gather | solution.py:132
  312.4 15.2 %all-to-all-start.1 = ((bf16[32,8,512]{2,1,0:T(8,128)(2,1)}), bf16[32,8,512]{2,1,0:T(8,128)(2,1)S(1)}, u32[]{:S(2)}, u32[]{:S(2)}) async-start(bf16[32,8,512]{2,1,0:T(8,128)(2,1)} %fusion.66), calls=%async_computation.1 | async-start | bytes 524288 | tf_op jit(solution)/shard_map/all_to_all | solution.py:64
  316.2 81.3 %all-gather.16.cloned.1.call-start = ((), (), s32[]{:S(2)}) async-start(), calls=%async_computation.20 | async-start | bytes 2162688 | tf_op jit(solution)/shard_map/all_gather | solution.py:132
  332.2 143.9 %reduce-scatter.30.cloned.1.call-start = ((), (), s32[]{:S(2)}) async-start(), calls=%async_computation.30 | async-start | bytes 540672
  368.3 188.4 %reduce-scatter.28.cloned.1.call-start = ((), (), s32[]{:S(2)}) async-start(), calls=%async_computation.29 | async-start | bytes 540672
  414.7 289.2 %reduce-scatter.16.cloned.1.call-start = ((), (), s32[]{:S(2)}) async-start(), calls=%async_computation.22 | async-start | bytes 2162688 | tf_op jit(solution)/shard_map/reduce_scatter | solution.py:153
  628.1 157.5 %reduce-scatter.18.cloned.1.call-start = ((), (), s32[]{:S(2)}) async-start(), calls=%async_computation.24 | async-start | bytes 2162688 | tf_op jit(solution)/shard_map/reduce_scatter | solution.py:153
  636.4 244.6 %reduce-scatter.32.cloned.1.call-start = ((), (), s32[]{:S(2)}) async-start(), calls=%async_computation.31 | async-start | bytes 81920
  704.0 82.9 %collective-permute-start.1 = (bf16[64,512]{1,0:T(8,128)(2,1)S(1)}, bf16[64,512]{1,0:T(8,128)(2,1)S(1)}, u32[]{:S(2)}, u32[]{:S(2)}) collective-permute-start(bf16[64,512]{1,0:T(8,128)(2,1)S(1)} %broadcast_select_fusion.1), channel_id=1, source_target_pairs={{64,0},{65,1},{66,2},{67,3},{68,4},{69,5},{70,6},{71,7},{72,8},{73... | collective-permute-start | bytes 196616 | tf_op jit(solution)/shard_map/ppermute | solution.py:12
  785.6 18.7 %collective-permute-start.3 = (bf16[64,512]{1,0:T(8,128)(2,1)S(1)}, bf16[64,512]{1,0:T(8,128)(2,1)S(1)}, u32[]{:S(2)}, u32[]{:S(2)}) collective-permute-start(bf16[64,512]{1,0:T(8,128)(2,1)S(1)} %broadcast_select_fusion), channel_id=1, source_target_pairs={{64,0},{65,1},{66,2},{67,3},{68,4},{69,5},{70,6},{71,7},{72,8},{73... | collective-permute-start | bytes 196616 | tf_op jit(solution)/shard_map/ppermute | solution.py:12
  787.9 17.4 %all-to-all-start.2 = ((bf16[32,8,512]{2,1,0:T(8,128)(2,1)}), bf16[32,8,512]{2,1,0:T(8,128)(2,1)S(1)}, u32[]{:S(2)}, u32[]{:S(2)}) async-start(bf16[32,8,512]{2,1,0:T(8,128)(2,1)} %fusion.73), calls=%async_computation.3 | async-start | bytes 524288 | tf_op jit(solution)/shard_map/all_to_all | solution.py:82
  795.2 191.5 %reduce-scatter.26.cloned.1.call-start = ((), (), s32[]{:S(2)}) async-start(), calls=%async_computation.28 | async-start | bytes 2293760 | tf_op jit(solution)/shard_map/reduce_scatter | solution.py:285
  805.2 16.4 %all-to-all-start.5 = ((bf16[32,8,512]{2,1,0:T(8,128)(2,1)}), bf16[32,8,512]{2,1,0:T(8,128)(2,1)S(1)}, u32[]{:S(2)}, u32[]{:S(2)}) async-start(bf16[32,8,512]{2,1,0:T(8,128)(2,1)} %fusion.75), calls=%async_computation.7 | async-start | bytes 524288 | tf_op jit(solution)/shard_map/all_to_all | solution.py:82
  812.6 174.0 %reduce-scatter.24.cloned.1.call-start = ((), (), s32[]{:S(2)}) async-start(), calls=%async_computation.27 | async-start | bytes 5242880 | tf_op jit(solution)/shard_map/reduce_scatter | solution.py:282
  828.6 195.0 %reduce-scatter.20.cloned.1.call-start = ((), (), s32[]{:S(2)}) async-start(), calls=%async_computation.25 | async-start | bytes 5242880 | tf_op jit(solution)/shard_map/reduce_scatter | solution.py:276
  846.4 259.9 %reduce-scatter.22.cloned.1.call-start = ((), (), s32[]{:S(2)}) async-start(), calls=%async_computation.26 | async-start | bytes 5242880 | tf_op jit(solution)/shard_map/reduce_scatter | solution.py:279
  860.8 14.7 %all-to-all-start.7 = ((bf16[32,8,512]{2,1,0:T(8,128)(2,1)}), bf16[32,8,512]{2,1,0:T(8,128)(2,1)S(1)}, u32[]{:S(2)}, u32[]{:S(2)}) async-start(bf16[32,8,512]{2,1,0:T(8,128)(2,1)} %fusion.56), calls=%async_computation.13 | async-start | bytes 524288 | tf_op jit(solution)/shard_map/all_to_all | solution.py:111
  875.5 14.4 %all-to-all-start.6 = ((bf16[32,8,512]{2,1,0:T(8,128)(2,1)}), bf16[32,8,512]{2,1,0:T(8,128)(2,1)S(1)}, u32[]{:S(2)}, u32[]{:S(2)}) async-start(bf16[32,8,512]{2,1,0:T(8,128)(2,1)} %fusion.61), calls=%async_computation.12 | async-start | bytes 524288 | tf_op jit(solution)/shard_map/all_to_all | solution.py:111
  (47 other events, 2067.2 us)
Sparse Core Ops, SparseCore 0:
  9.6 85.2 all-gather.11
  96.5 81.1 all-gather.9
  179.4 81.1 all-gather.13
  262.1 42.5 all-gather.17
  307.4 44.5 all-gather.19
  354.7 42.7 all-gather.15
  401.5 74.5 reduce-scatter.29
  480.1 76.5 reduce-scatter.27
  628.2 75.6 reduce-scatter.15
  707.3 78.1 reduce-scatter.17
  787.9 20.4 reduce-scatter.31
  811.3 43.6 reduce-scatter.25
  858.0 82.4 reduce-scatter.23
  943.3 80.2 reduce-scatter.19
  1026.5 79.7 reduce-scatter.21
where the time goes:
time: 1120 us; the launch traced here: 1110 us
  waiting for transfers between devices  688 us (61%)
  blocking collectives  170 us (15%)
  matrix products  138 us (12%)
  starting transfers between devices  54.4 us (5%)
  local copies, waits for them, and re-layouts  29.4 us (3%)
  other arithmetic  18.6 us (2%)
  between operations  14.8 us (1%)
    unnamed x18, waiting for transfers between devices  144 us
    reduce_scatter x2, waiting for transfers between devices, tower_step(): lax.psum_scatter(jnp.einsum('rtj,tdj->rd', grad_pre, w_in, preferred_elem...  129 us
    psum x1, blocking collectives, body(): grad_gain = lax.psum(trunk_sums[3], ('segment', 'expert', 'dp'))  96.5 us
    reduce_scatter x1, waiting for transfers between devices, body(): lax.psum_scatter(trunk_sums[1].astype(jnp.bfloat16), ('segment', 'dp'), s...  82.6 us
    all_gather x1, waiting for transfers between devices, body(): lax.all_gather(gate_weight, ('segment', 'dp'), axis=2, tiled=True)  77.4 us
    all_gather x1, waiting for transfers between devices, body(): lax.all_gather(down_weight, ('segment', 'dp'), axis=1, tiled=True)  76 us
    all_gather x1, waiting for transfers between devices, body(): lax.all_gather(up_weight, ('segment', 'dp'), axis=2, tiled=True)  61.7 us
    all_gather x2, blocking collectives, tower_step(): grad_value = lax.all_gather(grad_own, 'expert', axis=0, tiled=True)  48.9 us
  transfers between devices with their start and end apart: 26, of which 18 were waited for; matrix products, arithmetic and copies ran while one was open for 13% of the time, Pallas kernels for 0%

commit v1 on v0

v1 whole, which is shorter than its diff:
```python
import functools

import jax
import jax.numpy as jnp
from jax import lax
from jax.experimental import pallas as pl
from jax.experimental.pallas import tpu as pltpu
from jax.sharding import PartitionSpec as P

EPSILON = 1e-06
MESH = pl.DeviceIdType.MESH
VMEM = pltpu.VMEM
F32 = jnp.float32
BF16 = jnp.bfloat16


def place():
    return lax.axis_index("segment"), lax.axis_index("expert"), lax.axis_index("dp")


def remote(src, dst, send, recv, seg, expert, dp):
    return pltpu.make_async_remote_copy(
        src_ref=src,
        dst_ref=dst,
        send_sem=send,
        recv_sem=recv,
        device_id=(seg, expert, dp),
        device_id_type=MESH,
    )


def meet_plane(seg, me, dp, count):
    barrier = pltpu.get_barrier_semaphore()

    def greet(i, carry):
        pl.semaphore_signal(
            barrier, inc=1, device_id=(seg, lax.rem(me + i, count), dp), device_id_type=MESH
        )
        return carry

    lax.fori_loop(1, count, greet, 0)
    return barrier


def meet_all(seg, me, dp, count):
    barrier = pltpu.get_barrier_semaphore()
    all_count = 4 * count

    def greet(i, carry):
        e, z = i // 4, lax.rem(i, 4)
        pl.semaphore_signal(
            barrier,
            inc=1,
            device_id=(
                lax.rem(seg + lax.rem(z, 2), 2),
                lax.rem(me + e, count),
                lax.rem(dp + z // 2, 2),
            ),
            device_id_type=MESH,
        )
        return carry

    lax.fori_loop(1, all_count, greet, 0)
    pl.semaphore_wait(barrier, all_count - 1)


def wait_bytes(ref, sem):
    pltpu.make_async_copy(ref, ref, sem).wait()


def call(kernel, out_shape, scratch, ident, *args):
    return pl.pallas_call(
        kernel,
        out_shape=out_shape,
        in_specs=[pl.BlockSpec(memory_space=VMEM)] * len(args),
        out_specs=jax.tree.map(lambda _: pl.BlockSpec(memory_space=VMEM), out_shape),
        scratch_shapes=scratch,
        compiler_params=pltpu.CompilerParams(collective_id=ident, has_side_effects=True),
    )(*args)


def dispatch_kernel(count, slots, aux, got, got_aux, send, recv, aux_send, aux_recv):
    seg, me, dp = place()
    barrier = meet_plane(seg, me, dp, count)

    def greet(i, carry):
        pl.semaphore_signal(barrier, inc=1, device_id=(1 - seg, i, 1 - dp), device_id_type=MESH)
        return carry

    lax.fori_loop(0, count, greet, 0)
    pl.semaphore_wait(barrier, 2 * count - 1)
    mine = dp * count + me

    def start(i, carry):
        to = lax.rem(me + i, count)
        remote(slots.at[to], got.at[mine], send, recv, 1 - seg, to, 1 - dp).start()

        @pl.when(i > 0)
        def _():
            remote(slots.at[to], got.at[mine], send, recv, seg, to, dp).start()
            remote(aux, got_aux.at[me], aux_send, aux_recv, seg, to, dp).start()

        return carry

    lax.fori_loop(0, count, start, 0)
    pltpu.make_async_copy(slots.at[me], got.at[mine], recv).start()
    pltpu.make_async_copy(aux, got_aux.at[me], aux_recv).start()
    wait_bytes(got_aux, aux_recv)
    wait_bytes(got_aux.at[pl.ds(0, count - 1)], aux_send)
    wait_bytes(got, recv)
    wait_bytes(got.at[pl.ds(0, 2 * count - 1)], send)


def dispatch(slots, aux):
    count = slots.shape[0]
    return call(
        functools.partial(dispatch_kernel, count),
        (
            jax.ShapeDtypeStruct((2 * count,) + slots.shape[1:], slots.dtype),
            jax.ShapeDtypeStruct((count,) + aux.shape, aux.dtype),
        ),
        [pltpu.SemaphoreType.DMA(())] * 4,
        0,
        slots,
        aux,
    )


def giveback_kernel(count, sent, got, send, recv):
    seg, me, dp = place()
    meet_all(seg, me, dp, count)
    mine = (dp * 2 + seg) * count + me

    def start(i, carry):
        e, z = lax.rem(me + i // 4, count), lax.rem(i, 4)
        to_seg, to_dp = lax.rem(seg + lax.rem(z, 2), 2), lax.rem(dp + z // 2, 2)
        block = (to_dp * count + e) * 2 + to_seg
        remote(sent.at[block], got.at[mine], send, recv, to_seg, e, to_dp).start()
        return carry

    lax.fori_loop(1, 4 * count, start, 0)
    pltpu.make_async_copy(sent.at[(dp * count + me) * 2 + seg], got.at[mine], recv).start()
    wait_bytes(got, recv)
    wait_bytes(got.at[pl.ds(0, 4 * count - 1)], send)


def giveback(sent, count):
    return call(
        functools.partial(giveback_kernel, count),
        jax.ShapeDtypeStruct(sent.shape, sent.dtype),
        [pltpu.SemaphoreType.DMA(())] * 2,
        1,
        sent,
    )


def gather_kernel(count, rows, got, first_send, first_recv, pass_send, pass_recv):
    seg, me, dp = place()
    barrier = meet_plane(seg, me, dp, count)
    pl.semaphore_wait(barrier, count - 1)
    chips = count // 2
    chip, core = me // 2, lax.rem(me, 2)
    mine = core * chips + chip

    def start(i, carry):
        to = lax.rem(chip + i, chips)
        remote(rows, got.at[mine], first_send, first_recv.at[i], seg, to * 2 + core, dp).start()
        return carry

    lax.fori_loop(1, chips, start, 0)
    own = pltpu.make_async_copy(rows, got.at[mine], first_recv.at[0])
    own.start()
    remote(rows, got.at[mine], pass_send, pass_recv, seg, chip * 2 + 1 - core, dp).start()
    own.wait()

    def relay(i, carry):
        source = core * chips + lax.rem(chip - i + chips, chips)
        block = got.at[source]
        wait_bytes(block, first_recv.at[i])
        remote(block, block, pass_send, pass_recv, seg, chip * 2 + 1 - core, dp).start()
        return carry

    lax.fori_loop(1, chips, relay, 0)
    wait_bytes(got.at[pl.ds((1 - core) * chips, chips)], pass_recv)
    wait_bytes(got.at[pl.ds(0, chips)], pass_send)
    wait_bytes(got.at[pl.ds(0, chips - 1)], first_send)


def gather(rows, count):
    return call(
        functools.partial(gather_kernel, count),
        jax.ShapeDtypeStruct((count,) + rows.shape, rows.dtype),
        [
            pltpu.SemaphoreType.DMA(()),
            pltpu.SemaphoreType.DMA((count // 2,)),
            pltpu.SemaphoreType.DMA(()),
            pltpu.SemaphoreType.DMA(()),
        ],
        2,
        rows,
    )


def share_kernel(count, value, got, send, recv):
    seg, me, dp = place()
    barrier = meet_plane(seg, me, dp, count)
    pl.semaphore_wait(barrier, count - 1)

    def start(i, carry):
        to = lax.rem(me + i, count)
        remote(value, got.at[me], send, recv, seg, to, dp).start()
        return carry

    lax.fori_loop(1, count, start, 0)
    pltpu.make_async_copy(value, got.at[me], recv).start()
    wait_bytes(got, recv)
    wait_bytes(got.at[pl.ds(0, count - 1)], send)


def share(value, count):
    return call(
        functools.partial(share_kernel, count),
        jax.ShapeDtypeStruct((count,) + value.shape, value.dtype),
        [pltpu.SemaphoreType.DMA(())] * 2,
        3,
        value,
    )


def scatter_kernel(count, parts, out, pair, paired, got, pair_send, pair_recv, send, recv):
    seg, me, dp = place()
    barrier = meet_plane(seg, me, dp, count)
    pl.semaphore_wait(barrier, count - 1)
    chips = count // 2
    chip, core = me // 2, lax.rem(me, 2)

    def swap(i, carry):
        to = lax.rem(chip + chips - i, chips)
        remote(
            parts.at[(1 - core) * chips + to],
            pair.at[to],
            pair_send,
            pair_recv.at[to],
            seg,
            chip * 2 + 1 - core,
            dp,
        ).start()
        return carry

    lax.fori_loop(1, chips + 1, swap, 0)

    def forward(i, carry):
        to = lax.rem(chip + chips - i, chips)
        wait_bytes(pair.at[to], pair_recv.at[to])
        paired[to] = (
            parts[core * chips + to].astype(F32) + pair[to].astype(F32)
        ).astype(BF16)
        remote(paired.at[to], got.at[chip], send, recv, seg, to * 2 + core, dp).start()
        return carry

    lax.fori_loop(1, chips, forward, 0)
    wait_bytes(pair.at[chip], pair_recv.at[chip])
    got[chip] = (parts[core * chips + chip].astype(F32) + pair[chip].astype(F32)).astype(BF16)
    wait_bytes(got.at[pl.ds(0, chips - 1)], recv)
    total = got[0].astype(F32)
    for i in range(1, chips):
        total = total + got[i].astype(F32)
    out[...] = total.astype(BF16)
    wait_bytes(pair, pair_send)
    wait_bytes(got.at[pl.ds(0, chips - 1)], send)


def scatter(parts):
    count = parts.shape[0]
    half = (count // 2,) + parts.shape[1:]
    return call(
        functools.partial(scatter_kernel, count),
        jax.ShapeDtypeStruct(parts.shape[1:], parts.dtype),
        [
            pltpu.VMEM(half, BF16),
            pltpu.VMEM(half, BF16),
            pltpu.VMEM(half, BF16),
            pltpu.SemaphoreType.DMA(()),
            pltpu.SemaphoreType.DMA((count // 2,)),
            pltpu.SemaphoreType.DMA(()),
            pltpu.SemaphoreType.DMA(()),
        ],
        4,
        parts,
    )


def spread_kernel(count, slots, got, send, recv):
    seg, me, dp = place()
    meet_all(seg, me, dp, count)
    mine = (dp * count + me) * 2 + seg

    def start(i, carry):
        e, z = lax.rem(me + i // 4, count), lax.rem(i, 4)
        to_seg, to_dp = lax.rem(seg + lax.rem(z, 2), 2), lax.rem(dp + z // 2, 2)
        remote(slots.at[e], got.at[mine], send, recv, to_seg, e, to_dp).start()
        return carry

    lax.fori_loop(1, 4 * count, start, 0)
    pltpu.make_async_copy(slots.at[me], got.at[mine], recv).start()
    wait_bytes(got, recv)
    wait_bytes(got.at[pl.ds(0, 4 * count - 1)], send)


def spread(slots):
    count = slots.shape[0]
    return call(
        functools.partial(spread_kernel, count),
        jax.ShapeDtypeStruct((4 * count,) + slots.shape[1:], slots.dtype),
        [pltpu.SemaphoreType.DMA(())] * 2,
        5,
        slots,
    )


def add_all_kernel(count, part, out, got, send, recv):
    seg, me, dp = place()
    meet_all(seg, me, dp, count)
    mine = (dp * count + me) * 2 + seg

    def start(i, carry):
        e, z = lax.rem(me + i // 4, count), lax.rem(i, 4)
        to_seg, to_dp = lax.rem(seg + lax.rem(z, 2), 2), lax.rem(dp + z // 2, 2)
        remote(part, got.at[mine], send, recv, to_seg, e, to_dp).start()
        return carry

    lax.fori_loop(1, 4 * count, start, 0)
    pltpu.make_async_copy(part, got.at[mine], recv).start()
    wait_bytes(got, recv)
    out[...] = jnp.sum(got[...], axis=0)
    wait_bytes(got.at[pl.ds(0, 4 * count - 1)], send)


def add_all(part, count):
    return call(
        functools.partial(add_all_kernel, count),
        jax.ShapeDtypeStruct(part.shape, part.dtype),
        [
            pltpu.VMEM((4 * count,) + part.shape, part.dtype),
            pltpu.SemaphoreType.DMA(()),
            pltpu.SemaphoreType.DMA(()),
        ],
        6,
        part,
    )


def column_swap(value, over_segment, over_dp):
    pairs = []
    for s in range(2):
        for d in range(2):
            pairs.append((s * 2 + d, (s ^ over_segment) * 2 + (d ^ over_dp)))
    return lax.ppermute(value, ("segment", "dp"), pairs)


SWAPS = ((1, 0), (0, 1), (1, 1))


def slot_matrix(routes, experts, capacity):
    row_count, top_count = routes.shape
    flat_ids = routes.reshape(row_count * top_count)
    onehot = (flat_ids[:, None] == jnp.arange(experts, dtype=jnp.int32)[None, :]).astype(jnp.int32)
    before = jnp.cumsum(onehot, axis=0) - onehot
    slot_rank = jnp.sum(before * onehot, axis=1)
    position = flat_ids * capacity + slot_rank
    columns = jnp.arange(experts * capacity, dtype=jnp.int32)[None, :]
    slot_table = (position[:, None] == columns).astype(BF16)
    return jnp.sum(slot_table.reshape(row_count, top_count, experts * capacity), axis=1)


def mm(a, b, dims):
    return lax.dot_general(a, b, (dims, ((), ())), preferred_element_type=F32)


def body(
    features,
    routes,
    arm_ids,
    targets,
    trunk_gain,
    gate_weight,
    up_weight,
    down_weight,
    tower_in,
    tower_out,
):
    batches, rows_here, width = features.shape
    count = lax.axis_size("expert")
    experts = count
    capacity = max(2, 2 * routes.shape[2] * rows_here // experts)
    towers, _, piece = tower_in.shape
    loss_scale = float(batches * rows_here * count * lax.axis_size("dp")) ** (-0.5)
    seg = lax.axis_index("segment")
    w_gate, w_up, w_down = gate_weight[0], up_weight[0], down_weight[0]

    cols = towers * piece
    extra = jnp.zeros((16, cols), BF16).at[0].set(tower_out.reshape(cols))
    own = jnp.concatenate([tower_in.transpose(1, 0, 2).reshape(width, cols), extra], axis=0)
    pieces = [own] + [column_swap(own, *s) for s in SWAPS]

    wide_rows = features.astype(F32)
    scaled = wide_rows * lax.rsqrt(jnp.mean(wide_rows * wide_rows, axis=-1, keepdims=True) + EPSILON)
    normed = (scaled * trunk_gain).astype(BF16)
    tables = [slot_matrix(routes[b], experts, capacity) for b in range(batches)]
    outgoing = jnp.stack(
        [
            mm(tables[b], normed[b], ((0,), (0,))).astype(BF16).reshape(experts, capacity, width)
            for b in range(batches)
        ],
        axis=1,
    ).reshape(experts, batches * capacity, width)
    own_table = jnp.where(seg == 0, tables[0], tables[1])
    own_arms = jnp.where(seg == 0, arm_ids[0], arm_ids[1])
    own_targets = jnp.where(seg == 0, targets[0], targets[1])
    aux = jnp.concatenate([own_targets, own_arms.astype(F32)])[None, :]
    aux = jnp.broadcast_to(aux, (8, aux.shape[1]))
    inputs, aux_all = dispatch(outgoing, aux)
    inputs = inputs.reshape(-1, width)

    gate_pre = mm(inputs, w_gate, ((1,), (0,)))
    up_pre = mm(inputs, w_up, ((1,), (0,)))
    active = (jax.nn.silu(gate_pre) * up_pre).astype(BF16)
    produced = mm(active, w_down, ((1,), (0,))).astype(BF16)
    returned = giveback(produced.reshape(-1, capacity, width), count)
    table4 = jnp.concatenate([own_table] * 4, axis=1)
    added = mm(table4, returned.reshape(-1, width), ((1,), (0,)))
    own_rows = jnp.where(seg == 0, features[0], features[1])
    mixed = (own_rows.astype(F32) + added).astype(BF16)

    rows = gather(mixed, count).reshape(-1, width)
    packed = jnp.concatenate(pieces, axis=1)
    w_in = packed[:width]
    w_out = packed[width]
    column_tower = lax.rem(jnp.arange(4 * cols, dtype=jnp.int32), cols) // piece
    tower_mask = column_tower[:, None] == jnp.arange(8, dtype=jnp.int32)[None, :]
    out_matrix = jnp.where(tower_mask, w_out[:, None], jnp.zeros((), BF16))
    pre_act = mm(rows, w_in, ((1,), (0,)))
    sig = jax.nn.sigmoid(pre_act)
    hidden = (pre_act * sig).astype(BF16)
    slope = (sig * (1.0 + pre_act * (1.0 - sig))).astype(BF16)
    values = mm(hidden, out_matrix, ((1,), (0,)))
    aux_all = aux_all[:, 0, :].reshape(count // 2, 2, 2 * rows_here)
    aux_all = aux_all.transpose(1, 0, 2).reshape(count, 2, rows_here)
    all_targets = aux_all[:, 0].reshape(-1)
    all_arms = aux_all[:, 1].reshape(-1)
    arm_mask = all_arms[:, None] + 1.0 == jnp.arange(8, dtype=F32)[None, :]
    picked = jnp.sum(jnp.where(arm_mask, values, 0.0), axis=1)
    own_values = jnp.stack([values[:, 0], picked]).astype(BF16).reshape(-1, 128)
    summed = jnp.sum(share(own_values, count).astype(F32), axis=0).reshape(2, -1)
    treated = (all_arms != 0.0).astype(F32)
    grad_first = loss_scale * (jax.nn.sigmoid(summed[0]) - treated)
    grad_arm = loss_scale * (summed[1] - all_targets)
    first_mask = jnp.arange(8, dtype=jnp.int32)[None, :] == 0
    grad_value = jnp.where(first_mask, grad_first[:, None], jnp.where(arm_mask, grad_arm[:, None], 0.0))
    grad_value = grad_value.astype(BF16)
    spread_value = mm(grad_value, out_matrix, ((1,), (1,)))
    grad_pre = (spread_value * slope.astype(F32)).astype(BF16)
    part_rows = mm(grad_pre, w_in, ((1,), (1,))).astype(BF16)
    grad_rows = scatter(part_rows.reshape(count, rows_here, width))

    part_in = mm(rows, grad_pre, ((0,), (0,))).astype(BF16)
    part_out = mm(grad_value, hidden, ((0,), (0,)))
    part_out = jnp.sum(jnp.where(tower_mask.T, part_out, 0.0), axis=0)
    extra = jnp.zeros((16, 4 * cols), BF16).at[0].set(part_out.astype(BF16))
    parts = jnp.concatenate([part_in, extra], axis=0)
    tower_sum = parts[:, :cols].astype(F32)
    for k, s in enumerate(SWAPS):
        sent = parts[:, (k + 1) * cols : (k + 2) * cols]
        tower_sum = tower_sum + column_swap(sent, *s).astype(F32)
    tower_sum = tower_sum.astype(BF16)
    grad_tower_in = tower_sum[:width].reshape(width, towers, piece).transpose(1, 0, 2)
    grad_tower_out = tower_sum[width].reshape(towers, piece)

    back_slots = mm(own_table, grad_rows, ((0,), (0,))).astype(BF16)
    grads = spread(back_slots.reshape(experts, capacity, width)).reshape(-1, width)
    grad_active = mm(grads, w_down, ((1,), (1,)))
    sig = jax.nn.sigmoid(gate_pre)
    grad_gate_pre = (grad_active * up_pre * (sig * (1.0 + gate_pre * (1.0 - sig)))).astype(BF16)
    grad_up_pre = (grad_active * (gate_pre * sig)).astype(BF16)
    sum_gate = mm(inputs, grad_gate_pre, ((0,), (0,)))
    sum_up = mm(inputs, grad_up_pre, ((0,), (0,)))
    sum_down = mm(active, grads, ((0,), (0,)))
    gain_part = jnp.sum(sum_gate * w_gate.astype(F32) + sum_up * w_up.astype(F32), axis=1)
    gain_part = jnp.zeros((8, 128), F32).at[:4].set((gain_part / trunk_gain).reshape(4, 128))
    grad_gain = add_all(gain_part, count)[:4].reshape(width)
    return (
        sum_gate.astype(BF16)[None],
        sum_up.astype(BF16)[None],
        sum_down.astype(BF16)[None],
        grad_tower_in,
        grad_tower_out,
        grad_gain,
    )


def solution(mesh):
    in_specs = (
        P(None, ("expert", "dp"), None),
        P(None, ("expert", "dp"), None),
        P(None, ("expert", "dp")),
        P(None, ("expert", "dp")),
        P(),
        P("expert", None, ("segment", "dp")),
        P("expert", None, ("segment", "dp")),
        P("expert", ("segment", "dp"), None),
        P(None, None, ("segment", "expert", "dp")),
        P(None, ("segment", "expert", "dp")),
    )
    out_specs = (
        P("expert", None, ("segment", "dp")),
        P("expert", None, ("segment", "dp")),
        P("expert", ("segment", "dp"), None),
        P(None, None, ("segment", "expert", "dp")),
        P(None, ("segment", "expert", "dp")),
        P(),
    )
    return jax.shard_map(body, mesh=mesh, in_specs=in_specs, out_specs=out_specs, check_vma=False)
```

time: 1120 us -> 273 us (0.24)
  waiting for transfers between devices: 688 us -> 0.02 us
  Pallas kernels: 0 us -> 170 us
  blocking collectives: 170 us -> 0 us
  matrix products: 138 us -> 61.1 us
  starting transfers between devices: 54.4 us -> 8.76 us
  between operations: 14.8 us -> 1.05 us
    all_gather x6 -> x0, waiting for transfers between devices: 264 us -> none  [the longest x1 77.4 us: body(): lax.all_gather(gate_weight, ('segment', 'dp'), axis=2, tiled=True)]
    reduce_scatter x6 -> x0, waiting for transfers between devices: 248 us -> none  [the longest x2 129 us: tower_step(): lax.psum_scatter(jnp.einsum('rtj,tdj->rd', grad_pre, w_in, preferred_elem...]
    pallas_call x0 -> x7, Pallas kernels: none -> 170 us  [call(): pl.pallas_call(kernel, out_shape=out_shape, in_specs=[pl.BlockSpec(memory...]
    unnamed x18 -> x0, waiting for transfers between devices: 144 us -> none
    psum x1 -> x0, blocking collectives: 96.5 us -> none  [body(): grad_gain = lax.psum(trunk_sums[3], ('segment', 'expert', 'dp'))]
    dot_general x36 -> x17, matrix products: 138 us -> 61.1 us  [mm(): return lax.dot_general(a, b, (dims, ((), ())), preferred_element_type=F32)]
    all_gather x3 -> x0, blocking collectives: 60.1 us -> none  [the longest x2 48.9 us: tower_step(): grad_value = lax.all_gather(grad_own, 'expert', axis=0, tiled=True)]
    all_to_all x7 -> x0, starting transfers between devices: 46 us -> none  [the longest x2 14.7 us: trunk_backward(): lax.all_to_all(outgoing.reshape(experts, capacity, feature_width), 'exper...]
  transfers between devices with their start and end apart: 26 -> 6, of which waited for: 18 -> 0; matrix products, arithmetic and copies ran while one was open for 13% -> 12% of each run, Pallas kernels for 0% -> 39%
where the time goes in v1:
time: 273 us; the launch traced here: 271 us
  Pallas kernels  170 us (62%)
  matrix products  61.1 us (22%)
  local copies, waits for them, and re-layouts  19.5 us (7%)
  other arithmetic  10.8 us (4%)
  starting transfers between devices  8.76 us (3%)
    pallas_call x7, Pallas kernels, call(): pl.pallas_call(kernel, out_shape=out_shape, in_specs=[pl.BlockSpec(memory...  170 us
    dot_general x17, matrix products, mm(): return lax.dot_general(a, b, (dims, ((), ())), preferred_element_type=F32)  61.1 us
    ppermute x6, starting transfers between devices, column_swap(): return lax.ppermute(value, ('segment', 'dp'), pairs)  8.76 us
  transfers between devices with their start and end apart: 6, of which 0 were waited for; matrix products, arithmetic and copies ran while one was open for 12% of the time, Pallas kernels for 39%

profile of v1, /device:TPU:1, one launch (start us, length us, event | category | flops | bytes accessed | tf_op | source)
XLA Modules:
  0.0 271.1 jit_solution(3563640943654839533)
XLA Ops:
  2.8 4.7 %collective-permute-start.2 = (bf16[528,448]{1,0:T(8,128)(2,1)S(1)}, bf16[528,448]{1,0:T(8,128)(2,1)S(1)}, u32[]{:S(2)}, u32[]{:S(2)}) collective-permute-start(bf16[528,448]{1,0:T(8,128)(2,1)S(1)} %fusion.34), channel_id=1, source_target_pairs={{0,65},{1,64},{64,1},{65,0},{2,67},{3,66},{66,3},{67,2},{4,69},{5,... | collective-permute-start | bytes 1419272 | tf_op jit(solution)/shard_map/ppermute | solution.py:358
  17.1 26.9 %shard_map.145 = (bf16[64,16,512]{2,1,0:T(8,128)(2,1)}, f32[32,8,128]{2,1,0:T(8,128)}) custom-call(bf16[32,16,512]{2,1,0:T(8,128)(2,1)} %maximum_bitcast_fusion.slots, f32[8,128]{1,0:T(8,128)} %broadcast_in_dim.80.aux), custom_call_target="tpu_custom_call" | custom-call | tf_op jit(solution)/shard_map/pallas_call | solution.py:72
  45.4 2.9 %fusion.24 = f32[1024,1024]{1,0:T(8,128)S(1)} fusion(bf16[1024,512]{1,0:T(8,128)(2,1)} %bitcast.114, bf16[1,512,1024]{2,1,0:T(8,128)(2,1)} %param.21), kind=kOutput, calls=%fused_computation.45 | convolution fusion | flops 1073741824 | bytes 6291456 | tf_op jit(solution)/shard_map/dot_general | solution.py:377
  48.4 3.6 %multiply_convert_fusion.5 = (bf16[1024,1024]{1,0:T(8,128)(2,1)S(1)}, f32[1024,1024]{1,0:T(8,128)}) fusion(f32[1024,1024]{1,0:T(8,128)S(1)} %fusion.24, bf16[1024,512]{1,0:T(8,128)(2,1)S(1)} %bitcast.115, bf16[1,512,1024]{2,1,0:T(8,128)(2,1)S(1)} %copy-done.9), kind=kOutput, calls=%fused_computation.6 | convolution fusion | flops 1080033280 | bytes 12582912 | tf_op jit(solution)/shard_map/dot_general | solution.py:377
  53.2 2.2 fusion.8.sent
  55.5 29.5 %shard_map.146 = bf16[128,8,512]{2,1,0:T(8,128)(2,1)} custom-call(bf16[128,8,512]{2,1,0:T(8,128)(2,1)} %fusion.8.sent), custom_call_target="tpu_custom_call" | custom-call | tf_op jit(solution)/shard_map/pallas_call | solution.py:72
  85.0 2.2 fusion.13.rows
  87.2 26.1 %shard_map.147 = bf16[32,64,512]{2,1,0:T(8,128)(2,1)} custom-call(bf16[64,512]{1,0:T(8,128)(2,1)} %fusion.13.rows), custom_call_target="tpu_custom_call" | custom-call | tf_op jit(solution)/shard_map/pallas_call | solution.py:72
  114.9 3.1 %concatenate.24 = bf16[528,1792]{1,0:T(8,128)(2,1)S(1)} concatenate(bf16[528,448]{1,0:T(8,128)(2,1)S(1)} %fusion.34, bf16[528,448]{1,0:T(8,128)(2,1)} %collective-permute-done, bf16[528,448]{1,0:T(8,128)(2,1)} %copy-done.5, bf16[528,448]{1,0:T(8,128)(2,1)} %copy-done.4), dimensions={1} | concatenate | bytes 3784704 | tf_op jit(solution)/shard_map/concatenate | solution.py:436
  118.0 10.7 %multiply_convert_fusion.2 = (bf16[2048,1792]{1,0:T(8,128)(2,1)S(1)}, f32[2048,1792]{1,0:T(8,128)}) fusion(bf16[2048,512]{1,0:T(8,128)(2,1)} %bitcast.107, bf16[528,1792]{1,0:T(8,128)(2,1)S(1)} %concatenate.24), kind=kOutput, calls=%fused_computation.2 | convolution fusion | flops 3776446464 | bytes 25952256 | tf_op jit(solution)/shard_map/dot_general | solution.py:377
  128.7 2.1 select_reduce_fusion
  132.3 13.2 %shard_map.148 = bf16[32,32,128]{2,1,0:T(8,128)(2,1)} custom-call(bf16[32,128]{1,0:T(8,128)(2,1)} %convert_element_type.156.value), custom_call_target="tpu_custom_call" | custom-call | tf_op jit(solution)/shard_map/pallas_call | solution.py:72
  146.5 4.2 %fusion.14 = bf16[1792]{0:T(1024)(128)(2,1)S(1)} fusion(bf16[2048,1792]{1,0:T(8,128)(2,1)} %copy-done.1, bf16[2048]{0:T(1024)(128)(2,1)S(1)} %get-tuple-element.56, bf16[2048]{0:T(1024)(128)(2,1)S(1)} %get-tuple-element.55, f32[2048]{0:T(1024)S(1)} %add.99, pred[8]{0:T(512)(128)(4,1)S(1)} %iota_compare_fusion.9, s32[1792]{0:T(1024)S(1)} %add_select_fusion), kind=kOutput, calls=%fused_computation.33 | convolution fusion | flops 58810624 | bytes 7367176 | tf_op jit(solution)/shard_map/dot_general | solution.py:377
  150.7 10.1 %multiply_convert_fusion = bf16[2048,1792]{1,0:T(8,128)(2,1)S(1)} fusion(f32[2048,1792]{1,0:T(8,128)} %get-tuple-element.64, s32[1792]{0:T(1024)S(1)} %add_select_fusion, bf16[1792]{0:T(1024)(128)(2,1)S(1)} %slice_reduce_fusion.1, bf16[2048]{0:T(1024)(128)(2,1)S(1)} %get-tuple-element.56, bf16[2048]{0:T(1024)(128)(2,1)S(1)} %get-tuple-element.55, ...), kind=kOutput, calls=%fused_computation | convolution fusion | flops 99168256 | bytes 22047240 | tf_op jit(solution)/shard_map/dot_general | solution.py:377
  160.9 5.2 %convolution_convert_fusion = bf16[512,1792]{1,0:T(8,128)(2,1)} fusion(bf16[2048,512]{1,0:T(8,128)(2,1)S(1)} %bitcast.108, bf16[2048,1792]{1,0:T(8,128)(2,1)S(1)} %multiply_convert_fusion), kind=kOutput, calls=%fused_computation.11 | convolution fusion | flops 3759013888 | bytes 11272192 | tf_op jit(solution)/shard_map/dot_general | solution.py:377
  166.0 5.5 %convolution_convert_fusion.1 = bf16[2048,512]{1,0:T(8,128)(2,1)} fusion(bf16[2048,1792]{1,0:T(8,128)(2,1)S(1)} %multiply_convert_fusion, bf16[528,1792]{1,0:T(8,128)(2,1)S(1)} %concatenate.24), kind=kOutput, calls=%fused_computation.12 | convolution fusion | flops 3759144960 | bytes 11272192 | tf_op jit(solution)/shard_map/dot_general | solution.py:377
  171.5 25.3 %shard_map.149 = bf16[64,512]{1,0:T(8,128)(2,1)} custom-call(bf16[32,64,512]{2,1,0:T(8,128)(2,1)} %bitcast.109), custom_call_target="tpu_custom_call" | custom-call | tf_op jit(solution)/shard_map/pallas_call | solution.py:72
  196.8 1.8 fusion.12.slots
  198.6 26.2 %shard_map.150 = bf16[128,8,512]{2,1,0:T(8,128)(2,1)} custom-call(bf16[32,8,512]{2,1,0:T(8,128)(2,1)} %fusion.12.slots), custom_call_target="tpu_custom_call" | custom-call | tf_op jit(solution)/shard_map/pallas_call | solution.py:72
  224.8 1.7 fusion.4
  228.3 1.9 collective-permute-start.5
  235.6 3.4 %add_reduce_fusion = (f32[512]{0:T(512)S(1)}, bf16[1,512,1024]{2,1,0:T(8,128)(2,1)}, bf16[1,512,1024]{2,1,0:T(8,128)(2,1)}) fusion(f32[512,1024]{1,0:T(8,128)S(1)} %fusion.2, bf16[1,512,1024]{2,1,0:T(8,128)(2,1)S(1)} %copy-done.10, bf16[1,512,1024]{2,1,0:T(8,128)(2,1)S(1)} %copy-done.8, bf16[1024,512]{1,0:T(8,128)(2,1)S(1)} %bitcast.117, ...), kind=kOutput, calls=%fused_computation.15 | convolution fusion | flops 1088421376 | bytes 19924992 | tf_op jit(solution)/shard_map/dot_general | solution.py:377
  239.6 22.8 %shard_map.151 = f32[8,128]{1,0:T(8,128)} custom-call(f32[8,128]{1,0:T(8,128)} %scatter.14.part), custom_call_target="tpu_custom_call" | custom-call | tf_op jit(solution)/shard_map/pallas_call | solution.py:72
  263.7 4.1 %fusion.9 = bf16[1,1024,512]{2,1,0:T(8,128)(2,1)} fusion(bf16[1024,1024]{1,0:T(8,128)(2,1)} %copy-done.15, bf16[128,8,512]{2,1,0:T(8,128)(2,1)} %shard_map.150), kind=kOutput, calls=%fused_computation.24 | convolution fusion | flops 1074266112 | bytes 4194304 | tf_op jit(solution)/shard_map/dot_general | solution.py:377
  (103 shorter events, 30.8 us)
Async XLA Ops:
  0.6 52.6 %copy-start = (bf16[1,1024,512]{2,1,0:T(8,128)(2,1)S(1)}, bf16[1,1024,512]{2,1,0:T(8,128)(2,1)}, u32[]{:S(2)}) copy-start(bf16[1,1024,512]{2,1,0:T(8,128)(2,1)} %param.23) | copy-start | bytes 3145732
  2.8 110.5 %collective-permute-start.2 = (bf16[528,448]{1,0:T(8,128)(2,1)S(1)}, bf16[528,448]{1,0:T(8,128)(2,1)S(1)}, u32[]{:S(2)}, u32[]{:S(2)}) collective-permute-start(bf16[528,448]{1,0:T(8,128)(2,1)S(1)} %fusion.34), channel_id=1, source_target_pairs={{0,65},{1,64},{64,1},{65,0},{2,67},{3,66},{66,3},{67,2},{4,69},{5,... | collective-permute-start | bytes 1419272 | tf_op jit(solution)/shard_map/ppermute | solution.py:358
  7.4 105.8 %collective-permute-start.1 = (bf16[528,448]{1,0:T(8,128)(2,1)S(1)}, bf16[528,448]{1,0:T(8,128)(2,1)S(1)}, u32[]{:S(2)}, u32[]{:S(2)}) collective-permute-start(bf16[528,448]{1,0:T(8,128)(2,1)S(1)} %fusion.34), channel_id=1, source_target_pairs={{0,1},{1,0},{64,65},{65,64},{2,3},{3,2},{66,67},{67,66},{4,5},{5,4... | collective-permute-start | bytes 1419272 | tf_op jit(solution)/shard_map/ppermute | solution.py:358
  7.4 107.4 %collective-permute-start = (bf16[528,448]{1,0:T(8,128)(2,1)S(1)}, bf16[528,448]{1,0:T(8,128)(2,1)}, u32[]{:S(2)}, u32[]{:S(2)}) collective-permute-start(bf16[528,448]{1,0:T(8,128)(2,1)S(1)} %fusion.34), channel_id=1, source_target_pairs={{0,64},{1,65},{64,0},{65,1},{2,66},{3,67},{66,2},{67,3},{4,68},{5,... | collective-permute-start | bytes 1419272 | tf_op jit(solution)/shard_map/ppermute | solution.py:358
  45.4 3.0 %copy-start.9 = (bf16[1,512,1024]{2,1,0:T(8,128)(2,1)S(1)}, bf16[1,512,1024]{2,1,0:T(8,128)(2,1)}, u32[]{:S(2)}) copy-start(bf16[1,512,1024]{2,1,0:T(8,128)(2,1)} %param.22) | copy-start | bytes 3145732
  45.4 3.0 %copy-start.11 = (bf16[64,16,512]{2,1,0:T(8,128)(2,1)S(1)}, bf16[64,16,512]{2,1,0:T(8,128)(2,1)}, u32[]{:S(2)}) copy-start(bf16[64,16,512]{2,1,0:T(8,128)(2,1)} %get-tuple-element.44) | copy-start | bytes 3145732
  48.4 3.6 %copy-start.13 = (f32[1024,1024]{1,0:T(8,128)}, f32[1024,1024]{1,0:T(8,128)S(1)}, u32[]{:S(2)}) copy-start(f32[1024,1024]{1,0:T(8,128)S(1)} %fusion.24) | copy-start | bytes 12582916
  51.9 1.3 copy-start.15
  53.2 31.8 %copy-start.6 = (bf16[2,64,512]{2,1,0:T(8,128)(2,1)S(1)}, bf16[2,64,512]{2,1,0:T(8,128)(2,1)}, u32[]{:S(2)}) copy-start(bf16[2,64,512]{2,1,0:T(8,128)(2,1)} %param.16) | copy-start | bytes 393220
  113.3 0.8 copy-start.4
  114.1 0.8 copy-start.5
  128.7 2.9 %copy-start.1 = (bf16[2048,1792]{1,0:T(8,128)(2,1)}, bf16[2048,1792]{1,0:T(8,128)(2,1)S(1)}, u32[]{:S(2)}) copy-start(bf16[2048,1792]{1,0:T(8,128)(2,1)S(1)} %get-tuple-element.63) | copy-start | bytes 22020100
  150.7 10.1 %copy-start.2 = (bf16[32,64,512]{2,1,0:T(8,128)(2,1)S(1)}, bf16[32,64,512]{2,1,0:T(8,128)(2,1)}, u32[]{:S(2)}) copy-start(bf16[32,64,512]{2,1,0:T(8,128)(2,1)} %shard_map.147) | copy-start | bytes 6291460
  224.8 6.7 %copy-start.3 = (bf16[128,8,512]{2,1,0:T(8,128)(2,1)S(1)}, bf16[128,8,512]{2,1,0:T(8,128)(2,1)}, u32[]{:S(2)}) copy-start(bf16[128,8,512]{2,1,0:T(8,128)(2,1)} %shard_map.150) | copy-start | bytes 3145732
  228.0 39.8 %collective-permute-start.3 = (bf16[528,448]{1,0:T(8,128)(2,1)}, bf16[528,448]{1,0:T(8,128)(2,1)}, u32[]{:S(2)}, u32[]{:S(2)}) collective-permute-start(bf16[528,448]{1,0:T(8,128)(2,1)} %get-tuple-element.52), channel_id=1, source_target_pairs={{0,64},{1,65},{64,0},{65,1},{2,66},{3,67},{66,2},{67,3},{4,68},{5,... | collective-permute-start | bytes 1419272 | tf_op jit(solution)/shard_map/ppermute | solution.py:358
  228.3 39.4 %collective-permute-start.5 = (bf16[528,448]{1,0:T(8,128)(2,1)}, bf16[528,448]{1,0:T(8,128)(2,1)}, u32[]{:S(2)}, u32[]{:S(2)}) collective-permute-start(bf16[528,448]{1,0:T(8,128)(2,1)} %get-tuple-element.53), channel_id=1, source_target_pairs={{0,65},{1,64},{64,1},{65,0},{2,67},{3,66},{66,3},{67,2},{4,69},{5,... | collective-permute-start | bytes 1419272 | tf_op jit(solution)/shard_map/ppermute | solution.py:358
  230.3 2.5 copy-start.12
  230.3 2.5 copy-start.14
  230.3 37.5 %collective-permute-start.4 = (bf16[528,448]{1,0:T(8,128)(2,1)S(1)}, bf16[528,448]{1,0:T(8,128)(2,1)}, u32[]{:S(2)}, u32[]{:S(2)}) collective-permute-start(bf16[528,448]{1,0:T(8,128)(2,1)S(1)} %get-tuple-element.54), channel_id=1, source_target_pairs={{0,1},{1,0},{64,65},{65,64},{2,3},{3,2},{66,67},{67,66},{4,5},{5,4... | collective-permute-start | bytes 1419272 | tf_op jit(solution)/shard_map/ppermute | solution.py:358
  232.8 1.4 copy-start.8
  232.8 1.5 copy-start.10
  232.8 2.8 %copy-start.16 = (f32[1024,1024]{1,0:T(8,128)S(1)}, f32[1024,1024]{1,0:T(8,128)}, u32[]{:S(2)}) copy-start(f32[1024,1024]{1,0:T(8,128)} %get-tuple-element.62) | copy-start | bytes 12582916
  235.6 3.4 %copy-start.7 = (f32[512]{0:T(512)S(1)}, f32[512]{0:T(512)}, u32[]{:S(2)}) copy-start(f32[512]{0:T(512)} %param.20) | copy-start | bytes 6148

commit v2 on v0

v2 whole, which is shorter than its diff:
```python
import functools

import jax
import jax.numpy as jnp
from jax import lax
from jax.experimental import pallas as pl
from jax.experimental.pallas import tpu as pltpu
from jax.sharding import PartitionSpec as P

EPSILON = 1e-06
MESH = pl.DeviceIdType.MESH
F32 = jnp.float32
BF16 = jnp.bfloat16
NN = (((1,), (0,)), ((), ()))
NT = (((1,), (1,)), ((), ()))
TN = (((0,), (0,)), ((), ()))


def mm(a, b, dims=NN):
    return lax.dot_general(a, b, dims, preferred_element_type=F32)


def wait_bytes(ref, sem):
    pltpu.make_async_copy(ref, ref, sem).wait()


def wide(block):
    depth, rows, width = block.shape
    return block.astype(F32).reshape(depth * rows, width).astype(BF16)


def step_kernel(
    loss_scale,
    feats,
    routes,
    aux,
    gain,
    w_gate,
    w_up,
    w_down,
    own_piece,
    out_gate,
    out_up,
    out_down,
    out_tower,
    out_gain,
    tables,
    outgoing,
    x_in,
    x_rows,
    x_turned,
    by_gate,
    by_up,
    active,
    active_turned,
    p_out,
    r_in,
    mixed,
    mixed_turned,
    aux_in,
    weights,
    hidden,
    slope,
    values,
    value_out,
    value_in,
    grad_turned,
    grad_column,
    d_out,
    d_in,
    b_out,
    g_in,
    g_rows,
    w_pair_out,
    w_pair_in,
    w_z_out,
    w_z_in,
    gain_a_out,
    gain_a_in,
    gain_b_out,
    gain_b_in,
    x_send,
    x_recv,
    aux_send,
    aux_recv,
    p_send,
    p_recv,
    m_send,
    m_recv,
    v_send,
    v_recv,
    d_send,
    d_recv,
    g_send,
    g_recv,
    wz_send,
    wz_recv,
    wp_send,
    wp_recv,
    tp_send,
    tp_recv,
    tz_send,
    tz_recv,
    ga_send,
    ga_recv,
    gb_send,
    gb_recv,
):
    seg, me, dp = lax.axis_index("segment"), lax.axis_index("expert"), lax.axis_index("dp")
    batches, rows_here, width = feats.shape
    count = x_in.shape[0] // 4
    chips = count // 2
    capacity = x_in.shape[1]
    hidden_here = w_gate.shape[1]
    slots = count * capacity
    chip, core = me // 2, lax.rem(me, 2)
    twin = chip * 2 + 1 - core
    z_mine = dp * 2 + seg
    side = 4
    quarter = rows_here * chips // side
    z_peers = {1: (1 - seg, dp), 2: (seg, 1 - dp), 3: (1 - seg, 1 - dp)}

    def remote(src, dst, send, recv, to_seg, expert, to_dp):
        return pltpu.make_async_remote_copy(
            src_ref=src,
            dst_ref=dst,
            send_sem=send,
            recv_sem=recv,
            device_id=(to_seg, expert, to_dp),
            device_id_type=MESH,
        )

    barrier = pltpu.get_barrier_semaphore()

    def greet(i, carry):
        e, z = i // 4, lax.rem(i, 4)
        pl.semaphore_signal(
            barrier,
            inc=1,
            device_id=(
                lax.rem(seg + lax.rem(z, 2), 2),
                lax.rem(me + e, count),
                lax.rem(dp + z // 2, 2),
            ),
            device_id_type=MESH,
        )
        return carry

    lax.fori_loop(1, 4 * count, greet, 0)

    row_ids = lax.broadcasted_iota(jnp.int32, (rows_here, rows_here), 0)
    col_ids = lax.broadcasted_iota(jnp.int32, (rows_here, rows_here), 1)
    lower = (col_ids < row_ids).astype(F32).astype(BF16)
    expert_ids = lax.broadcasted_iota(jnp.int32, (rows_here, count), 1)
    stretch_row = lax.broadcasted_iota(jnp.int32, (count, slots), 0)
    stretch_col = lax.broadcasted_iota(jnp.int32, (count, slots), 1)
    stretch = (stretch_col // capacity == stretch_row).astype(F32).astype(BF16)
    slot_ids = lax.rem(
        lax.broadcasted_iota(jnp.int32, (rows_here, slots), 1), capacity
    ).astype(F32)
    for b in range(batches):
        wide_rows = feats[b].astype(F32)
        scaled = wide_rows * lax.rsqrt(
            jnp.mean(wide_rows * wide_rows, axis=-1, keepdims=True) + EPSILON
        )
        normed = (scaled * gain[...]).astype(BF16)
        named = routes[b]
        taken = jnp.where(
            (named[:, 0:1] == expert_ids) | (named[:, 1:2] == expert_ids), 1.0, 0.0
        ).astype(BF16)
        rank = mm(lower, taken).astype(BF16)
        taken_wide = mm(taken, stretch)
        rank_wide = mm(rank, stretch)
        table = jnp.where((taken_wide > 0.5) & (rank_wide == slot_ids), 1.0, 0.0).astype(BF16)
        tables[b] = table
        outgoing[b] = mm(table, normed, TN).reshape(count, capacity, width).astype(BF16)
    weights[core] = own_piece[...]

    pl.semaphore_wait(barrier, 4 * count - 1)

    def dispatch(i, carry):
        to = lax.rem(me + i, count)
        for b in range(batches):
            mine = (dp * 2 + b) * count + me
            block = outgoing.at[b, to]
            remote(block, x_in.at[mine], x_send, x_recv.at[1], 1 - seg, to, 1 - dp).start()

            @pl.when(i > 0)
            def _():
                remote(block, x_in.at[mine], x_send, x_recv.at[0], seg, to, dp).start()

        return carry

    lax.fori_loop(0, count, dispatch, 0)
    for b in range(batches):
        pltpu.make_async_copy(
            outgoing.at[b, me], x_in.at[(dp * 2 + b) * count + me], x_recv.at[0]
        ).start()

    def send_weights(k):
        to_seg, to_dp = z_peers[k]
        remote(
            own_piece, weights.at[k * 2 + core], wz_send.at[k], wz_recv.at[k], to_seg, me, to_dp
        ).start()

    def relay_weights(k):
        block = weights.at[k * 2 + core]
        wait_bytes(block, wz_recv.at[k])
        remote(block, block, wp_send.at[k], wp_recv.at[k], seg, twin, dp).start()

    remote(own_piece, weights.at[core], wp_send.at[0], wp_recv.at[0], seg, twin, dp).start()
    send_weights(1)

    def send_aux(i, carry):
        to = lax.rem(chip + i, chips)
        remote(aux, aux_in.at[chip], aux_send, aux_recv, seg, to * 2 + core, dp).start()
        return carry

    lax.fori_loop(1, chips, send_aux, 0)
    aux_in[chip] = aux[...]

    def forward(j, carry):
        to_dp = lax.rem(dp + j // 2, 2)
        to_seg = lax.rem(j, 2)
        base = (to_dp * 2 + to_seg) * count

        @pl.when(j == 0)
        def _():
            wait_bytes(x_in.at[pl.ds(dp * 2 * count, 2 * count)], x_recv.at[0])

        @pl.when(j == 2)
        def _():
            wait_bytes(x_in.at[pl.ds((1 - dp) * 2 * count, 2 * count)], x_recv.at[1])

        here = pl.ds(pl.multiple_of(base * capacity, slots), slots)
        rows = wide(x_in[pl.ds(base, count)])
        x_rows[here] = rows
        gate_pre = mm(rows, w_gate[...])
        up_pre = mm(rows, w_up[...])
        sig = jax.nn.sigmoid(gate_pre)
        gated = gate_pre * sig
        act = (gated * up_pre).astype(BF16)
        by_up[here] = gated.astype(BF16)
        by_gate[here] = (up_pre * (sig * (1.0 + gate_pre * (1.0 - sig)))).astype(BF16)
        active[here] = act
        made = mm(act, w_down[...])
        p_out[pl.ds(base, count)] = made.reshape(count, capacity, width).astype(BF16)
        local = (to_dp == dp) & (to_seg == seg)

        def give(i, inner):
            e = lax.rem(me + i, count)

            @pl.when((i > 0) | jnp.logical_not(local))
            def _():
                remote(
                    p_out.at[base + e],
                    r_in.at[z_mine * count + me],
                    p_send,
                    p_recv,
                    to_seg,
                    e,
                    to_dp,
                ).start()

            return inner

        lax.fori_loop(0, count, give, 0)

        @pl.when(local)
        def _():
            pltpu.make_async_copy(
                p_out.at[base + me], r_in.at[z_mine * count + me], p_recv
            ).start()

        return carry

    lax.fori_loop(0, 4, forward, 0)
    relay_weights(1)

    def turn(j, carry):
        here = pl.ds(pl.multiple_of(j * slots, slots), slots)
        x_turned[:, here] = x_rows[here].T
        active_turned[:, here] = active[here].T
        return carry

    lax.fori_loop(0, 4, turn, 0)

    wait_bytes(r_in, p_recv)
    own_table = tables[seg]
    added = mm(own_table, wide(r_in[pl.ds(0, count)]))
    for z in range(1, 4):
        added = added + mm(own_table, wide(r_in[pl.ds(z * count, count)]))
    mixed[chip] = (feats[seg].astype(F32) + added).astype(BF16)

    def send_rows(i, carry):
        to = lax.rem(chip + i, chips)
        block = mixed.at[chip]
        remote(block, block, m_send, m_recv.at[chip // side], seg, to * 2 + core, dp).start()
        return carry

    lax.fori_loop(1, chips, send_rows, 0)
    send_weights(3)
    send_weights(2)

    depth = width
    tower_count = 8
    out_cols = own_piece.shape[1]
    per_tower = out_cols // tower_count
    mask_tower = lax.broadcasted_iota(jnp.int32, (16, out_cols), 0)
    mask_col = lax.broadcasted_iota(jnp.int32, (16, out_cols), 1) // per_tower
    tower_mask = mask_tower == mask_col

    def out_matrix(piece):
        tail = weights[piece, depth:, :].astype(F32)
        return jnp.where(tower_mask, tail[0:1, :], 0.0).astype(BF16)

    def tower_forward(piece, group, fresh):
        here = pl.ds(pl.multiple_of(group * quarter, quarter), quarter)
        blocks = mixed[pl.ds(group * side, side)]
        rows = blocks.reshape(quarter, width)
        pre_act = mm(rows, weights[piece, :depth, :])
        sig = jax.nn.sigmoid(pre_act)
        hid = (pre_act * sig).astype(BF16)
        hidden[piece, here] = hid
        slope[piece, here] = (sig * (1.0 + pre_act * (1.0 - sig))).astype(BF16)
        part = mm(out_matrix(piece), hid, NT)
        if fresh:
            values[:, here] = part
        else:
            values[:, here] += part

    wait_bytes(weights.at[0], wp_recv.at[0])
    for j, ahead in enumerate((0, 1, 3, 2)):
        group = lax.rem(chip // side + ahead, side)
        if ahead == 0:
            wait_bytes(mixed.at[pl.ds(0, side - 1)], m_recv.at[group])
        else:
            wait_bytes(mixed.at[pl.ds(0, side)], m_recv.at[group])
        if j == 0:
            wait_bytes(weights.at[0], wp_recv.at[1])
        tower_forward(0, group, True)

        def more(p, carry, group=group):
            tower_forward(p, group, False)
            return carry

        lax.fori_loop(1, 4, more, 0)
    for k in (3, 2):
        relay_weights(k)
        for turn_core in (core, 1 - core):
            if turn_core is not core:
                wait_bytes(weights.at[0], wp_recv.at[k])

            def more_groups(group, carry, piece=k * 2 + turn_core):
                tower_forward(piece, group, False)
                return carry

            lax.fori_loop(0, side, more_groups, 0)

    wait_bytes(aux_in.at[pl.ds(0, chips - 1)], aux_recv)
    pairs = [aux_in[2 * g] + aux_in[2 * g + 1] for g in range(chips // 2)]
    notes = jnp.concatenate(pairs, axis=1)
    all_targets, all_arms = notes[0:1], notes[1:2]
    all_rows = chips * rows_here
    tower_ids = lax.broadcasted_iota(jnp.int32, (16, all_rows), 0).astype(F32)
    arm_mask = tower_ids - 1.0 == all_arms
    every = values[...]
    value_out[0:1] = every[0:1]
    value_out[1:2] = jnp.sum(jnp.where(arm_mask, every, 0.0), axis=0, keepdims=True)

    def send_values(i, carry):
        to = lax.rem(chip + i, chips)
        remote(value_out, value_in.at[chip], v_send, v_recv, seg, to * 2 + core, dp).start()
        return carry

    lax.fori_loop(1, chips, send_values, 0)
    value_in[chip] = value_out[...]
    for g in range(side):
        mixed_turned[:, g * quarter : (g + 1) * quarter] = (
            mixed[g * side : (g + 1) * side].reshape(quarter, width).T
        )
    wait_bytes(value_in.at[pl.ds(0, chips - 1)], v_recv)
    summed = value_in[0]
    for i in range(1, chips):
        summed = summed + value_in[i]
    treated = jnp.where(all_arms != 0.0, 1.0, 0.0)
    grad_first = loss_scale * (jax.nn.sigmoid(summed[0:1]) - treated)
    grad_arm = loss_scale * (summed[1:2] - all_targets)
    grad_value = jnp.where(tower_ids == 0.0, grad_first, jnp.where(arm_mask, grad_arm, 0.0))
    grad_turned[...] = grad_value.astype(BF16)
    grad_column[...] = grad_value.T.astype(BF16)

    def tower_back(j, carry):
        group = lax.rem(chip // side + 2 + j, side)
        here = pl.ds(pl.multiple_of(group * quarter, quarter), quarter)

        def one(p, total):
            spread_value = mm(grad_column[here], out_matrix(p))
            grad_pre = (spread_value * slope[p, here].astype(F32)).astype(BF16)
            slope[p, here] = grad_pre
            return total + mm(grad_pre, weights[p, :depth, :], NT)

        def two(p, total):
            return one(2 * p + 1, one(2 * p, total))

        total = lax.fori_loop(0, 4, two, jnp.zeros((quarter, width), F32))
        d_out[pl.ds(group * side, side)] = total.astype(BF16).reshape(side, rows_here, width)

        def send_grads(i, inner):
            to = group * side + i

            @pl.when(to != chip)
            def _():
                remote(
                    d_out.at[to], d_in.at[chip], d_send, d_recv, seg, to * 2 + core, dp
                ).start()

            return inner

        lax.fori_loop(0, side, send_grads, 0)
        return carry

    lax.fori_loop(0, side, tower_back, 0)
    d_in[chip] = d_out[chip]

    def tower_weight_grad(piece):
        main = mm(mixed_turned[...], slope[piece])
        tail = mm(grad_turned[...], hidden[piece])
        tail = jnp.sum(jnp.where(tower_mask, tail, 0.0), axis=0, keepdims=True)
        tail = jnp.where(mask_tower == 0, tail, 0.0)
        return main, tail

    def twin_grads(i, carry):
        k = 3 - i
        main, tail = tower_weight_grad(k * 2 + 1 - core)
        w_pair_out[k, :depth, :] = main.astype(BF16)
        w_pair_out[k, depth:, :] = tail.astype(BF16)
        remote(
            w_pair_out.at[k], w_pair_in.at[k], tp_send, tp_recv.at[k], seg, twin, dp
        ).start()
        return carry

    lax.fori_loop(0, 4, twin_grads, 0)

    wait_bytes(d_in.at[pl.ds(0, chips - 1)], d_recv)
    total = d_in[0].astype(F32)
    for i in range(1, chips):
        total = total + d_in[i].astype(F32)
    b_out[...] = mm(own_table, total.astype(BF16), TN).reshape(count, capacity, width).astype(BF16)

    def spread(i, carry):
        e, z = lax.rem(me + i // 4, count), lax.rem(i, 4)
        to_seg, to_dp = lax.rem(seg + lax.rem(z, 2), 2), lax.rem(dp + z // 2, 2)
        remote(
            b_out.at[e], g_in.at[z_mine * count + me], g_send, g_recv.at[z_mine], to_seg, e, to_dp
        ).start()
        return carry

    lax.fori_loop(1, 4 * count, spread, 0)
    pltpu.make_async_copy(b_out.at[me], g_in.at[z_mine * count + me], g_recv.at[z_mine]).start()

    for k in (3, 2, 1, 0):
        main, tail = tower_weight_grad(k * 2 + core)
        wait_bytes(w_pair_in.at[k], tp_recv.at[k])
        main = main + w_pair_in[k, :depth, :].astype(F32)
        tail = tail + w_pair_in[k, depth:, :].astype(F32)
        w_z_out[k, :depth, :] = main.astype(BF16)
        w_z_out[k, depth:, :] = tail.astype(BF16)
        if k:
            to_seg, to_dp = z_peers[k]
            remote(
                w_z_out.at[k], w_z_in.at[k], tz_send.at[k], tz_recv.at[k], to_seg, me, to_dp
            ).start()

    def backward(j, carry):
        z = lax.rem(z_mine + j, 4)
        wait_bytes(g_in.at[pl.ds(z * count, count)], g_recv.at[z])
        here = pl.ds(pl.multiple_of(z * slots, slots), slots)
        grads = wide(g_in[pl.ds(z * count, count)])
        g_rows[here] = grads
        grad_active = mm(grads, w_down[...], NT)
        by_gate[here] = (grad_active * by_gate[here].astype(F32)).astype(BF16)
        by_up[here] = (grad_active * by_up[here].astype(F32)).astype(BF16)
        return carry

    lax.fori_loop(0, 4, backward, 0)
    strip = 256

    def gate_grads(j, total):
        cols = pl.ds(pl.multiple_of(j * strip, strip), strip)
        for source, weight, out in ((by_gate, w_gate, out_gate), (by_up, w_up, out_up)):
            grad = mm(x_turned[...], source[:, cols])
            out[:, cols] = grad.astype(BF16)
            term = grad * weight[:, cols].astype(F32)
            for c in range(strip // 128):
                total = total + term[:, c * 128 : (c + 1) * 128]
        return total

    gain_sum = lax.fori_loop(0, hidden_here // strip, gate_grads, jnp.zeros((width, 128), F32))
    gain_row = jnp.sum(gain_sum.T, axis=0, keepdims=True)
    gain_a_out[...] = gain_row / gain[...]
    mine_a = z_mine * 2 + core
    others = []
    for flip_seg in range(2):
        for flip_dp in range(2):
            for flip_core in range(2):
                if flip_seg or flip_dp or flip_core:
                    others.append((flip_seg, flip_dp, flip_core))
    for flip_seg, flip_dp, flip_core in others:
        remote(
            gain_a_out,
            gain_a_in.at[mine_a],
            ga_send,
            ga_recv,
            1 - seg if flip_seg else seg,
            twin if flip_core else me,
            1 - dp if flip_dp else dp,
        ).start()
    gain_a_in[mine_a] = gain_a_out[...]

    def down_grads(j, carry):
        here = pl.ds(pl.multiple_of(j * strip, strip), strip)
        out_down[here] = mm(active_turned[here], g_rows[...]).astype(BF16)
        return carry

    half = hidden_here // strip // 2
    lax.fori_loop(0, half, down_grads, 0)
    wait_bytes(gain_a_in.at[pl.ds(0, 7)], ga_recv)
    part = gain_a_in[0]
    for i in range(1, 8):
        part = part + gain_a_in[i]
    gain_b_out[...] = part

    def send_gain(i, carry):
        to = lax.rem(chip + i, chips)
        remote(gain_b_out, gain_b_in.at[chip], gb_send, gb_recv, seg, to * 2 + core, dp).start()
        return carry

    lax.fori_loop(1, chips, send_gain, 0)
    gain_b_in[chip] = gain_b_out[...]
    lax.fori_loop(half, hidden_here // strip, down_grads, 0)

    tower_sum = w_z_out[0].astype(F32)
    for k in (1, 3, 2):
        wait_bytes(w_z_in.at[k], tz_recv.at[k])
        tower_sum = tower_sum + w_z_in[k].astype(F32)
    out_tower[...] = tower_sum.astype(BF16)
    wait_bytes(gain_b_in.at[pl.ds(0, chips - 1)], gb_recv)
    part = gain_b_in[0]
    for i in range(1, chips):
        part = part + gain_b_in[i]
    out_gain[...] = part

    wait_bytes(x_in.at[pl.ds(0, 4 * count - 2)], x_send)
    wait_bytes(aux_in.at[pl.ds(0, chips - 1)], aux_send)
    wait_bytes(r_in.at[pl.ds(0, 4 * count - 1)], p_send)
    wait_bytes(mixed.at[pl.ds(0, chips - 1)], m_send)
    wait_bytes(value_in.at[pl.ds(0, chips - 1)], v_send)
    wait_bytes(d_in.at[pl.ds(0, chips - 1)], d_send)
    wait_bytes(g_in.at[pl.ds(0, 4 * count - 1)], g_send)
    for k in range(1, 4):
        wait_bytes(own_piece, wz_send.at[k])
        wait_bytes(own_piece, tz_send.at[k])
    for k in range(4):
        wait_bytes(own_piece, wp_send.at[k])
    wait_bytes(w_pair_in, tp_send)
    wait_bytes(gain_a_in.at[pl.ds(0, 7)], ga_send)
    wait_bytes(gain_b_in.at[pl.ds(0, chips - 1)], gb_send)


def run_step(loss_scale, count, capacity, feats, routes, aux, gain, w_gate, w_up, w_down, piece):
    batches, rows_here, width = feats.shape
    hidden_here = w_gate.shape[1]
    chips = count // 2
    blocks = 4 * count
    slots = blocks * capacity
    all_rows = chips * rows_here
    cols = piece.shape[1]
    v = pltpu.VMEM
    dma = pltpu.SemaphoreType.DMA
    scratch = [
        v((batches, rows_here, count * capacity), BF16),
        v((batches, count, capacity, width), BF16),
        v((blocks, capacity, width), BF16),
        v((slots, width), BF16),
        v((width, slots), BF16),
        v((slots, hidden_here), BF16),
        v((slots, hidden_here), BF16),
        v((slots, hidden_here), BF16),
        v((hidden_here, slots), BF16),
        v((blocks, capacity, width), BF16),
        v((blocks, capacity, width), BF16),
        v((chips, rows_here, width), BF16),
        v((width, all_rows), BF16),
        v((chips, 8, 128), F32),
        v((8,) + piece.shape, BF16),
        v((8, all_rows, cols), BF16),
        v((8, all_rows, cols), BF16),
        v((16, all_rows), F32),
        v((2, all_rows), F32),
        v((chips, 2, all_rows), F32),
        v((16, all_rows), BF16),
        v((all_rows, 16), BF16),
        v((chips, rows_here, width), BF16),
        v((chips, rows_here, width), BF16),
        v((count, capacity, width), BF16),
        v((blocks, capacity, width), BF16),
        v((slots, width), BF16),
        v((4,) + piece.shape, BF16),
        v((4,) + piece.shape, BF16),
        v((4,) + piece.shape, BF16),
        v((4,) + piece.shape, BF16),
        v((1, width), F32),
        v((8, 1, width), F32),
        v((1, width), F32),
        v((chips, 1, width), F32),
        dma(()),
        dma((2,)),
        dma(()),
        dma(()),
        dma(()),
        dma(()),
        dma(()),
        dma((4,)),
        dma(()),
        dma(()),
        dma(()),
        dma(()),
        dma(()),
        dma((4,)),
        dma((4,)),
        dma((4,)),
        dma((4,)),
        dma((4,)),
        dma(()),
        dma((4,)),
        dma((4,)),
        dma((4,)),
        dma(()),
        dma(()),
        dma(()),
        dma(()),
    ]
    out_shape = (
        jax.ShapeDtypeStruct(w_gate.shape, BF16),
        jax.ShapeDtypeStruct(w_up.shape, BF16),
        jax.ShapeDtypeStruct(w_down.shape, BF16),
        jax.ShapeDtypeStruct(piece.shape, BF16),
        jax.ShapeDtypeStruct((1, width), F32),
    )
    spec = pl.BlockSpec(memory_space=pltpu.VMEM)
    return pl.pallas_call(
        functools.partial(step_kernel, loss_scale),
        out_shape=out_shape,
        in_specs=[spec] * 8,
        out_specs=(spec,) * 5,
        scratch_shapes=scratch,
        compiler_params=pltpu.CompilerParams(
            collective_id=0, has_side_effects=True, vmem_limit_bytes=67043328
        ),
    )(feats, routes, aux, gain, w_gate, w_up, w_down, piece)


def body(
    features,
    routes,
    arm_ids,
    targets,
    trunk_gain,
    gate_weight,
    up_weight,
    down_weight,
    tower_in,
    tower_out,
):
    batches, rows_here, width = features.shape
    count = lax.axis_size("expert")
    capacity = max(2, 2 * routes.shape[2] * rows_here // count)
    towers, _, piece = tower_in.shape
    loss_scale = float(batches * rows_here * count * lax.axis_size("dp")) ** (-0.5)
    seg = lax.axis_index("segment")
    odd = lax.rem(lax.axis_index("expert") // 2, 2)
    cols = 8 * piece
    turned = tower_in.transpose(1, 0, 2).reshape(width, towers * piece)
    own = jnp.zeros((width + 16, cols), BF16)
    own = own.at[:width, : towers * piece].set(turned)
    own = own.at[width, : towers * piece].set(tower_out.reshape(towers * piece))
    notes = jnp.stack(
        [
            jnp.where(seg == 0, targets[0], targets[1]),
            jnp.where(seg == 0, arm_ids[0], arm_ids[1]).astype(F32),
        ]
    )
    blank = jnp.zeros_like(notes)
    aux = jnp.concatenate(
        [jnp.where(odd == 0, notes, blank), jnp.where(odd == 0, blank, notes)], axis=1
    )
    aux = jnp.concatenate([aux, jnp.zeros((6, 2 * rows_here), F32)], axis=0)
    grad_gate, grad_up, grad_down, grad_tower, grad_gain = run_step(
        loss_scale,
        count,
        capacity,
        features,
        routes,
        aux,
        trunk_gain.reshape(1, width),
        gate_weight[0],
        up_weight[0],
        down_weight[0],
        own,
    )
    grad_tower_in = grad_tower[:width, : towers * piece].reshape(width, towers, piece)
    return (
        grad_gate[None],
        grad_up[None],
        grad_down[None],
        grad_tower_in.transpose(1, 0, 2),
        grad_tower[width, : towers * piece].reshape(towers, piece),
        grad_gain.reshape(width),
    )


def solution(mesh):
    in_specs = (
        P(None, ("expert", "dp"), None),
        P(None, ("expert", "dp"), None),
        P(None, ("expert", "dp")),
        P(None, ("expert", "dp")),
        P(),
        P("expert", None, ("segment", "dp")),
        P("expert", None, ("segment", "dp")),
        P("expert", ("segment", "dp"), None),
        P(None, None, ("segment", "expert", "dp")),
        P(None, ("segment", "expert", "dp")),
    )
    out_specs = (
        P("expert", None, ("segment", "dp")),
        P("expert", None, ("segment", "dp")),
        P("expert", ("segment", "dp"), None),
        P(None, None, ("segment", "expert", "dp")),
        P(None, ("segment", "expert", "dp")),
        P(),
    )
    return jax.shard_map(body, mesh=mesh, in_specs=in_specs, out_specs=out_specs, check_vma=False)
```

time: 1120 us -> 170 us (0.15)
  waiting for transfers between devices: 688 us -> 0 us
  blocking collectives: 170 us -> 0 us
  Pallas kernels: 0 us -> 154 us
  matrix products: 138 us -> 0 us
  starting transfers between devices: 54.4 us -> 0 us
  other arithmetic: 18.6 us -> 0.69 us
  local copies, waits for them, and re-layouts: 29.4 us -> 14.4 us
  between operations: 14.8 us -> 0.71 us
    all_gather x6 -> x0, waiting for transfers between devices: 264 us -> none  [the longest x1 77.4 us: body(): lax.all_gather(gate_weight, ('segment', 'dp'), axis=2, tiled=True)]
    reduce_scatter x6 -> x0, waiting for transfers between devices: 248 us -> none  [the longest x2 129 us: tower_step(): lax.psum_scatter(jnp.einsum('rtj,tdj->rd', grad_pre, w_in, preferred_elem...]
    pallas_call x0 -> x1, Pallas kernels: none -> 154 us  [run_step(): pl.pallas_call(functools.partial(step_kernel, loss_scale), out_shape=out_...]
    unnamed x18 -> x0, waiting for transfers between devices: 144 us -> none
    dot_general x36 -> x0, matrix products: 138 us -> none  [the longest x2 21.3 us: tower_step(): jnp.einsum('rd,tdj->rtj', row_piece, w_in, preferred_element_type=jnp.flo...]
    psum x1 -> x0, blocking collectives: 96.5 us -> none  [body(): grad_gain = lax.psum(trunk_sums[3], ('segment', 'expert', 'dp'))]
    all_gather x3 -> x0, blocking collectives: 60.1 us -> none  [the longest x2 48.9 us: tower_step(): grad_value = lax.all_gather(grad_own, 'expert', axis=0, tiled=True)]
    all_to_all x7 -> x0, starting transfers between devices: 46 us -> none  [the longest x2 14.7 us: trunk_backward(): lax.all_to_all(outgoing.reshape(experts, capacity, feature_width), 'exper...]
  transfers between devices with their start and end apart: 26 -> 0, of which waited for: 18 -> 0; matrix products, arithmetic and copies ran while one was open for 13% -> 0% of each run, Pallas kernels for 0% -> 0%
where the time goes in v2:
time: 170 us
  Pallas kernels  154 us (91%)
  local copies, waits for them, and re-layouts  14.4 us (8%)
    pallas_call x1, Pallas kernels, run_step(): pl.pallas_call(functools.partial(step_kernel, loss_scale), out_shape=out_...  154 us
    unnamed x21, local copies, waits for them, and re-layouts  7.45 us

profile of v2, /device:TPU:1, one launch (start us, length us, event | category | flops | bytes accessed | tf_op | source)
XLA Modules:
  0.0 169.9 jit_solution(6265744547381489530)
XLA Ops:
  0.7 0.0 copy-start.6
  0.7 0.7 copy-done.6
  1.3 0.7 copy-done.7
  2.0 0.0 copy-start.4
  2.0 0.7 select_maximum_fusion.aux
  2.7 0.0 copy-done.4
  2.7 0.1 reshape.87
  2.8 0.6 copy-done.3
  3.4 0.7 copy.20.routes
  4.1 1.2 copy.19
  5.4 0.9 scatter.6
  6.2 1.3 scatter.9.own_piece
  7.5 154.0 %shard_map.145 = (bf16[512,1024]{1,0:T(8,128)(2,1)}, bf16[512,1024]{1,0:T(8,128)(2,1)}, bf16[1024,512]{1,0:T(8,128)(2,1)}, bf16[528,512]{1,0:T(8,128)(2,1)}, f32[1,512]{1,0:T(1,128)}) custom-call(bf16[2,64,512]{2,1,0:T(8,128)(2,1)} %feats.1, s32[2,64,2]{2,1,0:T(8,128)} %copy.20.routes, f32[8,128]{1,0:T(8,128)} %select_maximum_fusion.aux, f32[1,512]{1,0:T(1,128)} %bitcast.22, ...), custom_call_target="tpu_custom_call" | custom-call | tf_op jit(solution)/shard_map/pallas_call | solution.py:652
  161.6 0.0 copy-start.2
  161.6 0.8 slice_reduce_fusion
  162.4 1.1 slice.61
  163.5 1.0 copy.21
  164.4 0.7 reshape_squeeze.3
  165.1 1.0 copy.27
  166.1 0.6 copy-done.1
  166.7 1.0 copy.28
  167.7 0.6 copy-done
  168.3 1.0 copy.29
  169.3 0.6 copy.30
  (10 shorter events, 0.0 us)
Async XLA Ops:
  0.7 0.7 copy-start.6
  1.3 0.7 copy-start.7
  2.0 0.7 copy-start.4
  2.7 0.7 copy-start.3
  161.6 3.5 %copy-start.2 = (bf16[512,1024]{1,0:T(8,128)(2,1)S(1)}, bf16[512,1024]{1,0:T(8,128)(2,1)}, u32[]{:S(2)}) copy-start(bf16[512,1024]{1,0:T(8,128)(2,1)} %get-tuple-element.35) | copy-start | bytes 3145732
  165.1 1.6 copy-start.1
  166.7 1.6 copy-start
  168.3 1.0 copy-start.5

commit v3 on v2

--- a/solution.py
+++ b/solution.py
@@ -24,6 +24,10 @@
     pltpu.make_async_copy(ref, ref, sem).wait()
 
 
+def sigmoid(value):
+    return 0.5 * jnp.tanh(0.5 * value) + 0.5
+
+
 def wide(block):
     depth, rows, width = block.shape
     return block.astype(F32).reshape(depth * rows, width).astype(BF16)
@@ -33,25 +37,31 @@
     loss_scale,
     feats,
     routes,
-    aux,
+    arms,
+    targets,
     gain,
     w_gate,
     w_up,
     w_down,
-    own_piece,
+    tower_in,
+    tower_out,
     out_gate,
     out_up,
     out_down,
     out_tower,
+    out_tower_row,
     out_gain,
+    aux,
+    own_piece,
+    tail_row,
+    sum_row,
+    grad_wide,
     tables,
     outgoing,
     x_in,
-    x_rows,
     x_turned,
     by_gate,
     by_up,
-    active,
     active_turned,
     p_out,
     r_in,
@@ -111,7 +121,10 @@
     count = x_in.shape[0] // 4
     chips = count // 2
     capacity = x_in.shape[1]
+    w_gate, w_up, w_down = w_gate.at[0], w_up.at[0], w_down.at[0]
+    out_gate, out_up, out_down = out_gate.at[0], out_up.at[0], out_down.at[0]
     hidden_here = w_gate.shape[1]
+    towers, _, per_tower = tower_in.shape
     slots = count * capacity
     chip, core = me // 2, lax.rem(me, 2)
     twin = chip * 2 + 1 - core
@@ -146,7 +159,7 @@
         )
         return carry
 
-    lax.fori_loop(1, 4 * count, greet, 0)
+    lax.fori_loop(1, 4 * count, greet, 0, unroll=8)
 
     row_ids = lax.broadcasted_iota(jnp.int32, (rows_here, rows_here), 0)
     col_ids = lax.broadcasted_iota(jnp.int32, (rows_here, rows_here), 1)
@@ -174,7 +187,24 @@
         table = jnp.where((taken_wide > 0.5) & (rank_wide == slot_ids), 1.0, 0.0).astype(BF16)
         tables[b] = table
         outgoing[b] = mm(table, normed, TN).reshape(count, capacity, width).astype(BF16)
+    own_piece[...] = jnp.zeros_like(own_piece)
+    tail_row[...] = jnp.zeros_like(tail_row)
+    for t in range(towers):
+        here = slice(t * per_tower, (t + 1) * per_tower)
+        own_piece[:width, here] = tower_in[t]
+        tail_row[0:1, here] = tower_out[t : t + 1, :].astype(F32)
+    own_piece[width:, :] = tail_row[...].astype(BF16)
     weights[core] = own_piece[...]
+    aux[...] = jnp.zeros_like(aux)
+    own_targets = jnp.where(seg == 0, targets[0:1, :], targets[1:2, :])
+    own_arms = jnp.where(seg == 0, arms[0:1, :], arms[1:2, :]).astype(F32)
+    for odd in range(2):
+
+        @pl.when(lax.rem(chip, 2) == odd)
+        def _():
+            aux[0:1, odd * rows_here : (odd + 1) * rows_here] = own_targets
+            aux[1:2, odd * rows_here : (odd + 1) * rows_here] = own_arms
+
 
     pl.semaphore_wait(barrier, 4 * count - 1)
 
@@ -234,15 +264,16 @@
 
         here = pl.ds(pl.multiple_of(base * capacity, slots), slots)
         rows = wide(x_in[pl.ds(base, count)])
-        x_rows[here] = rows
         gate_pre = mm(rows, w_gate[...])
         up_pre = mm(rows, w_up[...])
-        sig = jax.nn.sigmoid(gate_pre)
+        sig = sigmoid(gate_pre)
         gated = gate_pre * sig
         act = (gated * up_pre).astype(BF16)
         by_up[here] = gated.astype(BF16)
-        by_gate[here] = (up_pre * (sig * (1.0 + gate_pre * (1.0 - sig)))).astype(BF16)
-        active[here] = act
+        by_gate[here] = (up_pre * (sig + gated - gated * sig)).astype(BF16)
+        half_hidden = hidden_here // 2
+        hidden[0, here] = act[:, :half_hidden]
+        hidden[1, here] = act[:, half_hidden:]
         made = mm(act, w_down[...])
         p_out[pl.ds(base, count)] = made.reshape(count, capacity, width).astype(BF16)
         local = (to_dp == dp) & (to_seg == seg)
@@ -275,12 +306,14 @@
         return carry
 
     lax.fori_loop(0, 4, forward, 0)
+    send_weights(3)
     relay_weights(1)
 
     def turn(j, carry):
         here = pl.ds(pl.multiple_of(j * slots, slots), slots)
-        x_turned[:, here] = x_rows[here].T
-        active_turned[:, here] = active[here].T
+        x_turned[:, here] = wide(x_in[pl.ds(j * count, count)]).T
+        active_turned[: hidden_here // 2, here] = hidden[0, here].T
+        active_turned[hidden_here // 2 :, here] = hidden[1, here].T
         return carry
 
     lax.fori_loop(0, 4, turn, 0)
@@ -299,13 +332,9 @@
         return carry
 
     lax.fori_loop(1, chips, send_rows, 0)
-    send_weights(3)
-    send_weights(2)
 
     depth = width
-    tower_count = 8
     out_cols = own_piece.shape[1]
-    per_tower = out_cols // tower_count
     mask_tower = lax.broadcasted_iota(jnp.int32, (16, out_cols), 0)
     mask_col = lax.broadcasted_iota(jnp.int32, (16, out_cols), 1) // per_tower
     tower_mask = mask_tower == mask_col
@@ -319,10 +348,12 @@
         blocks = mixed[pl.ds(group * side, side)]
         rows = blocks.reshape(quarter, width)
         pre_act = mm(rows, weights[piece, :depth, :])
-        sig = jax.nn.sigmoid(pre_act)
-        hid = (pre_act * sig).astype(BF16)
+        sig = sigmoid(pre_act)
+        hid_wide = pre_act * sig
+        hid = hid_wide.astype(BF16)
         hidden[piece, here] = hid
-        slope[piece, here] = (sig * (1.0 + pre_act * (1.0 - sig))).astype(BF16)
+        tail = weights[piece, depth:, :].astype(F32)[0:1, :]
+        slope[piece, here] = ((sig + hid_wide - hid_wide * sig) * tail).astype(BF16)
         part = mm(out_matrix(piece), hid, NT)
         if fresh:
             values[:, here] = part
@@ -345,8 +376,20 @@
             return carry
 
         lax.fori_loop(1, 4, more, 0)
+        if j == 0:
+            relay_weights(3)
+            remote(
+                weights.at[6 + core],
+                weights.at[4 + core],
+                wz_send.at[2],
+                wz_recv.at[2],
+                1 - seg,
+                me,
+                dp,
+            ).start()
     for k in (3, 2):
-        relay_weights(k)
+        if k == 2:
+            relay_weights(2)
         for turn_core in (core, 1 - core):
             if turn_core is not core:
                 wait_bytes(weights.at[0], wp_recv.at[k])
@@ -384,19 +427,22 @@
     for i in range(1, chips):
         summed = summed + value_in[i]
     treated = jnp.where(all_arms != 0.0, 1.0, 0.0)
-    grad_first = loss_scale * (jax.nn.sigmoid(summed[0:1]) - treated)
+    grad_first = loss_scale * (sigmoid(summed[0:1]) - treated)
     grad_arm = loss_scale * (summed[1:2] - all_targets)
     grad_value = jnp.where(tower_ids == 0.0, grad_first, jnp.where(arm_mask, grad_arm, 0.0))
     grad_turned[...] = grad_value.astype(BF16)
     grad_column[...] = grad_value.T.astype(BF16)
+    mask_row = jnp.where(tower_mask, 1.0, 0.0).astype(BF16)
+    for g in range(side):
+        here = slice(g * quarter, (g + 1) * quarter)
+        grad_wide[here] = mm(grad_column[here], mask_row).astype(BF16)
 
     def tower_back(j, carry):
         group = lax.rem(chip // side + 2 + j, side)
         here = pl.ds(pl.multiple_of(group * quarter, quarter), quarter)
 
         def one(p, total):
-            spread_value = mm(grad_column[here], out_matrix(p))
-            grad_pre = (spread_value * slope[p, here].astype(F32)).astype(BF16)
+            grad_pre = grad_wide[here] * slope[p, here]
             slope[p, here] = grad_pre
             return total + mm(grad_pre, weights[p, :depth, :], NT)
 
@@ -431,7 +477,7 @@
         return main, tail
 
     def twin_grads(i, carry):
-        k = 3 - i
+        k = lax.rem(2 + 3 * i, 4)
         main, tail = tower_weight_grad(k * 2 + 1 - core)
         w_pair_out[k, :depth, :] = main.astype(BF16)
         w_pair_out[k, depth:, :] = tail.astype(BF16)
@@ -442,6 +488,21 @@
 
     lax.fori_loop(0, 4, twin_grads, 0)
 
+    def send_piece(k, to, slot):
+        remote(
+            w_z_out.at[k], w_z_in.at[slot], tz_send.at[slot], tz_recv.at[slot], *to
+        ).start()
+
+    for k in (2, 1, 0, 3):
+        main, tail = tower_weight_grad(k * 2 + core)
+        wait_bytes(w_pair_in.at[k], tp_recv.at[k])
+        main = main + w_pair_in[k, :depth, :].astype(F32)
+        tail = tail + w_pair_in[k, depth:, :].astype(F32)
+        w_z_out[k, :depth, :] = main.astype(BF16)
+        w_z_out[k, depth:, :] = tail.astype(BF16)
+        if k == 2:
+            send_piece(2, (1 - seg, me, dp), 2)
+
     wait_bytes(d_in.at[pl.ds(0, chips - 1)], d_recv)
     total = d_in[0].astype(F32)
     for i in range(1, chips):
@@ -459,18 +520,10 @@
     lax.fori_loop(1, 4 * count, spread, 0)
     pltpu.make_async_copy(b_out.at[me], g_in.at[z_mine * count + me], g_recv.at[z_mine]).start()
 
-    for k in (3, 2, 1, 0):
-        main, tail = tower_weight_grad(k * 2 + core)
-        wait_bytes(w_pair_in.at[k], tp_recv.at[k])
-        main = main + w_pair_in[k, :depth, :].astype(F32)
-        tail = tail + w_pair_in[k, depth:, :].astype(F32)
-        w_z_out[k, :depth, :] = main.astype(BF16)
-        w_z_out[k, depth:, :] = tail.astype(BF16)
-        if k:
-            to_seg, to_dp = z_peers[k]
-            remote(
-                w_z_out.at[k], w_z_in.at[k], tz_send.at[k], tz_recv.at[k], to_seg, me, to_dp
-            ).start()
+    send_piece(1, (1 - seg, me, dp), 1)
+    wait_bytes(w_z_in.at[2], tz_recv.at[2])
+    w_z_out[3] = (w_z_out[3].astype(F32) + w_z_in[2].astype(F32)).astype(BF16)
+    send_piece(3, (1 - seg, me, 1 - dp), 3)
 
     def backward(j, carry):
         z = lax.rem(z_mine + j, 4)
@@ -541,10 +594,14 @@
     lax.fori_loop(half, hidden_here // strip, down_grads, 0)
 
     tower_sum = w_z_out[0].astype(F32)
-    for k in (1, 3, 2):
+    for k in (1, 3):
         wait_bytes(w_z_in.at[k], tz_recv.at[k])
         tower_sum = tower_sum + w_z_in[k].astype(F32)
-    out_tower[...] = tower_sum.astype(BF16)
+    for t in range(towers):
+        here = slice(t * per_tower, (t + 1) * per_tower)
+        out_tower[t] = tower_sum[:width, here].astype(BF16)
+        sum_row[t : t + 1, :] = tower_sum[width : width + 1, here]
+    out_tower_row[...] = sum_row[0:towers, :].astype(BF16)
     wait_bytes(gain_b_in.at[pl.ds(0, chips - 1)], gb_recv)
     part = gain_b_in[0]
     for i in range(1, chips):
@@ -568,23 +625,28 @@
     wait_bytes(gain_b_in.at[pl.ds(0, chips - 1)], gb_send)
 
 
-def run_step(loss_scale, count, capacity, feats, routes, aux, gain, w_gate, w_up, w_down, piece):
+def run_step(loss_scale, count, capacity, *args):
+    feats, routes, arms, targets, gain, w_gate, w_up, w_down, tower_in, tower_out = args
     batches, rows_here, width = feats.shape
-    hidden_here = w_gate.shape[1]
+    hidden_here = w_gate.shape[2]
+    cols = 8 * tower_in.shape[2]
+    piece = jax.ShapeDtypeStruct((width + 16, cols), BF16)
     chips = count // 2
     blocks = 4 * count
     slots = blocks * capacity
     all_rows = chips * rows_here
-    cols = piece.shape[1]
     v = pltpu.VMEM
     dma = pltpu.SemaphoreType.DMA
     scratch = [
+        v((8, 2 * rows_here), F32),
+        v(piece.shape, BF16),
+        v((16, cols), F32),
+        v((8, tower_in.shape[2]), F32),
+        v((all_rows, cols), BF16),
         v((batches, rows_here, count * capacity), BF16),
         v((batches, count, capacity, width), BF16),
         v((blocks, capacity, width), BF16),
-        v((slots, width), BF16),
         v((width, slots), BF16),
-        v((slots, hidden_here), BF16),
         v((slots, hidden_here), BF16),
         v((slots, hidden_here), BF16),
         v((hidden_here, slots), BF16),
@@ -645,20 +707,21 @@
         jax.ShapeDtypeStruct(w_gate.shape, BF16),
         jax.ShapeDtypeStruct(w_up.shape, BF16),
         jax.ShapeDtypeStruct(w_down.shape, BF16),
-        jax.ShapeDtypeStruct(piece.shape, BF16),
+        jax.ShapeDtypeStruct(tower_in.shape, BF16),
+        jax.ShapeDtypeStruct(tower_out.shape, BF16),
         jax.ShapeDtypeStruct((1, width), F32),
     )
     spec = pl.BlockSpec(memory_space=pltpu.VMEM)
     return pl.pallas_call(
         functools.partial(step_kernel, loss_scale),
         out_shape=out_shape,
-        in_specs=[spec] * 8,
-        out_specs=(spec,) * 5,
+        in_specs=[spec] * len(args),
+        out_specs=(spec,) * len(out_shape),
         scratch_shapes=scratch,
         compiler_params=pltpu.CompilerParams(
             collective_id=0, has_side_effects=True, vmem_limit_bytes=67043328
         ),
-    )(feats, routes, aux, gain, w_gate, w_up, w_down, piece)
+    )(*args)
 
 
 def body(
@@ -676,48 +739,23 @@
     batches, rows_here, width = features.shape
     count = lax.axis_size("expert")
     capacity = max(2, 2 * routes.shape[2] * rows_here // count)
-    towers, _, piece = tower_in.shape
     loss_scale = float(batches * rows_here * count * lax.axis_size("dp")) ** (-0.5)
-    seg = lax.axis_index("segment")
-    odd = lax.rem(lax.axis_index("expert") // 2, 2)
-    cols = 8 * piece
-    turned = tower_in.transpose(1, 0, 2).reshape(width, towers * piece)
-    own = jnp.zeros((width + 16, cols), BF16)
-    own = own.at[:width, : towers * piece].set(turned)
-    own = own.at[width, : towers * piece].set(tower_out.reshape(towers * piece))
-    notes = jnp.stack(
-        [
-            jnp.where(seg == 0, targets[0], targets[1]),
-            jnp.where(seg == 0, arm_ids[0], arm_ids[1]).astype(F32),
-        ]
-    )
-    blank = jnp.zeros_like(notes)
-    aux = jnp.concatenate(
-        [jnp.where(odd == 0, notes, blank), jnp.where(odd == 0, blank, notes)], axis=1
-    )
-    aux = jnp.concatenate([aux, jnp.zeros((6, 2 * rows_here), F32)], axis=0)
-    grad_gate, grad_up, grad_down, grad_tower, grad_gain = run_step(
+    *grads, grad_gain = run_step(
         loss_scale,
         count,
         capacity,
         features,
         routes,
-        aux,
+        arm_ids,
+        targets,
         trunk_gain.reshape(1, width),
-        gate_weight[0],
-        up_weight[0],
-        down_weight[0],
-        own,
+        gate_weight,
+        up_weight,
+        down_weight,
+        tower_in,
+        tower_out,
     )
-    grad_tower_in = grad_tower[:width, : towers * piece].reshape(width, towers, piece)
-    return (
-        grad_gate[None],
-        grad_up[None],
-        grad_down[None],
-        grad_tower_in.transpose(1, 0, 2),
-        grad_tower[width, : towers * piece].reshape(towers, piece),
-        grad_gain.reshape(width),
-    )
+    return (*grads, grad_gain.reshape(width))
 
 
 def solution(mesh):

time: 170 us -> 162 us (0.953)
  Pallas kernels: 154 us -> 150 us
  local copies, waits for them, and re-layouts: 14.4 us -> 11.4 us
    pallas_call x1, Pallas kernels: 154 us -> 150 us  [run_step(): pl.pallas_call(functools.partial(step_kernel, loss_scale), out_shape=out_...]
    unnamed x21 -> x18, local copies, waits for them, and re-layouts: 7.45 us -> 11.4 us
    slice x3 -> x0, local copies, waits for them, and re-layouts: 2.84 us -> none  [the longest x2 2.04 us: body(): grad_tower[:width, :towers * piece].reshape(width, towers, piece)]
    scatter x2 -> x0, local copies, waits for them, and re-layouts: 2.17 us -> none  [the longest x1 1.32 us: body(): own = own.at[width, :towers * piece].set(tower_out.reshape(towers * piece))]
    another operation x3 -> x0, local copies, waits for them, and re-layouts: 1.96 us -> none
where the time goes in v3:
time: 162 us
  Pallas kernels  150 us (93%)
  local copies, waits for them, and re-layouts  11.4 us (7%)
    pallas_call x1, Pallas kernels, run_step(): pl.pallas_call(functools.partial(step_kernel, loss_scale), out_shape=out_...  150 us
    unnamed x18, local copies, waits for them, and re-layouts  11.4 us

profile of v3, /device:TPU:1, one launch (start us, length us, event | category | flops | bytes accessed | tf_op | source)
XLA Modules:
  0.0 161.8 jit_solution(16739486211059635771)
XLA Ops:
  0.6 1.4 copy.16.routes
  2.0 2.3 %copy.17.tower_in = bf16[7,512,64]{2,1,0:T(8,128)(2,1)} copy(bf16[7,512,64]{1,2,0:T(8,128)(2,1)} %param.18) | data formatting | bytes 917504 | tf_op args[8]
  4.3 149.7 %shard_map.145 = (bf16[1,512,1024]{2,1,0:T(8,128)(2,1)}, bf16[1,512,1024]{2,1,0:T(8,128)(2,1)}, bf16[1,1024,512]{2,1,0:T(8,128)(2,1)}, bf16[7,512,64]{2,1,0:T(8,...) custom-call(bf16[2,64,512]{2,1,0:T(8,128)(2,1)} %feats.1, s32[2,64,2]{2,1,0:T(8,128)} %copy.16.routes, s32[2,64]{1,0:T(2,128)} %arms.1, ...), custom_call_target="tpu_custom_call" | custom-call | tf_op jit(solution)/shard_map/pallas_call | solution.py:715
  154.0 0.0 copy-start.2
  154.1 2.3 %copy.18 = bf16[7,512,64]{1,2,0:T(8,128)(2,1)} copy(bf16[7,512,64]{2,1,0:T(8,128)(2,1)} %get-tuple-element.21) | data formatting | bytes 917504
  156.4 0.0 copy-done.2
  156.4 0.0 copy-start.1
  156.4 1.0 copy.24
  157.4 0.6 copy-done.1
  158.0 0.0 copy-start
  158.0 1.0 copy.25
  159.0 0.6 copy-done
  159.6 0.0 copy-start.4
  159.6 1.0 copy.26
  160.6 0.0 copy-done.4
  160.6 0.0 copy-start.3
  160.6 0.6 copy.27
  161.1 0.1 copy-done.3
  161.2 0.6 copy.28
Async XLA Ops:
  154.0 2.3 %copy-start.2 = (bf16[1,512,1024]{2,1,0:T(8,128)(2,1)S(1)}, bf16[1,512,1024]{2,1,0:T(8,128)(2,1)}, u32[]{:S(2)}) copy-start(bf16[1,512,1024]{2,1,0:T(8,128)(2,1)} %get-tuple-element.30) | copy-start | bytes 3145732
  156.4 1.6 copy-start.1
  158.0 1.6 copy-start
  159.6 1.0 copy-start.4
  160.6 0.7 copy-start.3

commit v4 on v3

--- a/solution.py
+++ b/solution.py
@@ -124,7 +124,7 @@
     w_gate, w_up, w_down = w_gate.at[0], w_up.at[0], w_down.at[0]
     out_gate, out_up, out_down = out_gate.at[0], out_up.at[0], out_down.at[0]
     hidden_here = w_gate.shape[1]
-    towers, _, per_tower = tower_in.shape
+    towers, per_tower, _ = tower_in.shape
     slots = count * capacity
     chip, core = me // 2, lax.rem(me, 2)
     twin = chip * 2 + 1 - core
@@ -164,7 +164,7 @@
     row_ids = lax.broadcasted_iota(jnp.int32, (rows_here, rows_here), 0)
     col_ids = lax.broadcasted_iota(jnp.int32, (rows_here, rows_here), 1)
     lower = (col_ids < row_ids).astype(F32).astype(BF16)
-    expert_ids = lax.broadcasted_iota(jnp.int32, (rows_here, count), 1)
+    expert_ids = lax.broadcasted_iota(jnp.int32, (count, rows_here), 0)
     stretch_row = lax.broadcasted_iota(jnp.int32, (count, slots), 0)
     stretch_col = lax.broadcasted_iota(jnp.int32, (count, slots), 1)
     stretch = (stretch_col // capacity == stretch_row).astype(F32).astype(BF16)
@@ -179,20 +179,59 @@
         normed = (scaled * gain[...]).astype(BF16)
         named = routes[b]
         taken = jnp.where(
-            (named[:, 0:1] == expert_ids) | (named[:, 1:2] == expert_ids), 1.0, 0.0
-        ).astype(BF16)
+            (named[0:1, :] == expert_ids) | (named[1:2, :] == expert_ids), 1.0, 0.0
+        )
+        taken = taken.T.astype(BF16)
         rank = mm(lower, taken).astype(BF16)
         taken_wide = mm(taken, stretch)
         rank_wide = mm(rank, stretch)
         table = jnp.where((taken_wide > 0.5) & (rank_wide == slot_ids), 1.0, 0.0).astype(BF16)
         tables[b] = table
         outgoing[b] = mm(table, normed, TN).reshape(count, capacity, width).astype(BF16)
-    own_piece[...] = jnp.zeros_like(own_piece)
+    pl.semaphore_wait(barrier, 4 * count - 1)
+
+    def dispatch_near(i, carry):
+        to = lax.rem(me + i, count)
+        for b in range(batches):
+            mine = (dp * 2 + b) * count + me
+            remote(
+                outgoing.at[b, to], x_in.at[mine], x_send, x_recv.at[0], seg, to, dp
+            ).start()
+        return carry
+
+    def dispatch_far(i, carry):
+        to = lax.rem(me + i, count)
+        for b in range(batches):
+            mine = (dp * 2 + b) * count + me
+            remote(
+                outgoing.at[b, to], x_in.at[mine], x_send, x_recv.at[1], 1 - seg, to, 1 - dp
+            ).start()
+        return carry
+
+    lax.fori_loop(1, count, dispatch_near, 0)
+    lax.fori_loop(0, count, dispatch_far, 0)
+    for b in range(batches):
+        pltpu.make_async_copy(
+            outgoing.at[b, me], x_in.at[(dp * 2 + b) * count + me], x_recv.at[0]
+        ).start()
+
+    def send_weights(k):
+        to_seg, to_dp = z_peers[k]
+        remote(
+            own_piece, weights.at[k * 2 + core], wz_send.at[k], wz_recv.at[k], to_seg, me, to_dp
+        ).start()
+
+    def relay_weights(k):
+        block = weights.at[k * 2 + core]
+        wait_bytes(block, wz_recv.at[k])
+        remote(block, block, wp_send.at[k], wp_recv.at[k], seg, twin, dp).start()
+
     tail_row[...] = jnp.zeros_like(tail_row)
     for t in range(towers):
-        here = slice(t * per_tower, (t + 1) * per_tower)
-        own_piece[:width, here] = tower_in[t]
-        tail_row[0:1, here] = tower_out[t : t + 1, :].astype(F32)
+        tail_row[0:1, t * per_tower : (t + 1) * per_tower] = tower_out[t : t + 1, :].astype(F32)
+    blank = jnp.zeros((own_piece.shape[1] - towers * per_tower, width), BF16)
+    stacked = jnp.concatenate([tower_in[t] for t in range(towers)] + [blank], axis=0)
+    own_piece[:width, :] = stacked.T
     own_piece[width:, :] = tail_row[...].astype(BF16)
     weights[core] = own_piece[...]
     aux[...] = jnp.zeros_like(aux)
@@ -204,39 +243,6 @@
         def _():
             aux[0:1, odd * rows_here : (odd + 1) * rows_here] = own_targets
             aux[1:2, odd * rows_here : (odd + 1) * rows_here] = own_arms
-
-
-    pl.semaphore_wait(barrier, 4 * count - 1)
-
-    def dispatch(i, carry):
-        to = lax.rem(me + i, count)
-        for b in range(batches):
-            mine = (dp * 2 + b) * count + me
-            block = outgoing.at[b, to]
-            remote(block, x_in.at[mine], x_send, x_recv.at[1], 1 - seg, to, 1 - dp).start()
-
-            @pl.when(i > 0)
-            def _():
-                remote(block, x_in.at[mine], x_send, x_recv.at[0], seg, to, dp).start()
-
-        return carry
-
-    lax.fori_loop(0, count, dispatch, 0)
-    for b in range(batches):
-        pltpu.make_async_copy(
-            outgoing.at[b, me], x_in.at[(dp * 2 + b) * count + me], x_recv.at[0]
-        ).start()
-
-    def send_weights(k):
-        to_seg, to_dp = z_peers[k]
-        remote(
-            own_piece, weights.at[k * 2 + core], wz_send.at[k], wz_recv.at[k], to_seg, me, to_dp
-        ).start()
-
-    def relay_weights(k):
-        block = weights.at[k * 2 + core]
-        wait_bytes(block, wz_recv.at[k])
-        remote(block, block, wp_send.at[k], wp_recv.at[k], seg, twin, dp).start()
 
     remote(own_piece, weights.at[core], wp_send.at[0], wp_recv.at[0], seg, twin, dp).start()
     send_weights(1)
@@ -306,7 +312,26 @@
         return carry
 
     lax.fori_loop(0, 4, forward, 0)
-    send_weights(3)
+    top = 272
+    halves = ((0, pl.ds(0, top)), (3, pl.ds(top, width + 16 - top)))
+    for sem, part in halves:
+        remote(
+            own_piece.at[part],
+            weights.at[6 + core, part],
+            wz_send.at[sem],
+            wz_recv.at[sem],
+            1 - seg,
+            me,
+            1 - dp,
+        ).start()
+
+    def relay_half(sem, part):
+        block = weights.at[6 + core, part]
+        wait_bytes(block, wz_recv.at[sem])
+        remote(
+            block, weights.at[4 + core, part], wz_send.at[2], wz_recv.at[2], 1 - seg, me, dp
+        ).start()
+
     relay_weights(1)
 
     def turn(j, carry):
@@ -318,6 +343,7 @@
 
     lax.fori_loop(0, 4, turn, 0)
 
+    relay_half(*halves[0])
     wait_bytes(r_in, p_recv)
     own_table = tables[seg]
     added = mm(own_table, wide(r_in[pl.ds(0, count)]))
@@ -332,6 +358,9 @@
         return carry
 
     lax.fori_loop(1, chips, send_rows, 0)
+    relay_half(*halves[1])
+    far = weights.at[6 + core]
+    remote(far, far, wp_send.at[3], wp_recv.at[3], seg, twin, dp).start()
 
     depth = width
     out_cols = own_piece.shape[1]
@@ -376,17 +405,6 @@
             return carry
 
         lax.fori_loop(1, 4, more, 0)
-        if j == 0:
-            relay_weights(3)
-            remote(
-                weights.at[6 + core],
-                weights.at[4 + core],
-                wz_send.at[2],
-                wz_recv.at[2],
-                1 - seg,
-                me,
-                dp,
-            ).start()
     for k in (3, 2):
         if k == 2:
             relay_weights(2)
@@ -437,38 +455,6 @@
         here = slice(g * quarter, (g + 1) * quarter)
         grad_wide[here] = mm(grad_column[here], mask_row).astype(BF16)
 
-    def tower_back(j, carry):
-        group = lax.rem(chip // side + 2 + j, side)
-        here = pl.ds(pl.multiple_of(group * quarter, quarter), quarter)
-
-        def one(p, total):
-            grad_pre = grad_wide[here] * slope[p, here]
-            slope[p, here] = grad_pre
-            return total + mm(grad_pre, weights[p, :depth, :], NT)
-
-        def two(p, total):
-            return one(2 * p + 1, one(2 * p, total))
-
-        total = lax.fori_loop(0, 4, two, jnp.zeros((quarter, width), F32))
-        d_out[pl.ds(group * side, side)] = total.astype(BF16).reshape(side, rows_here, width)
-
-        def send_grads(i, inner):
-            to = group * side + i
-
-            @pl.when(to != chip)
-            def _():
-                remote(
-                    d_out.at[to], d_in.at[chip], d_send, d_recv, seg, to * 2 + core, dp
-                ).start()
-
-            return inner
-
-        lax.fori_loop(0, side, send_grads, 0)
-        return carry
-
-    lax.fori_loop(0, side, tower_back, 0)
-    d_in[chip] = d_out[chip]
-
     def tower_weight_grad(piece):
         main = mm(mixed_turned[...], slope[piece])
         tail = mm(grad_turned[...], hidden[piece])
@@ -476,32 +462,75 @@
         tail = jnp.where(mask_tower == 0, tail, 0.0)
         return main, tail
 
-    def twin_grads(i, carry):
-        k = lax.rem(2 + 3 * i, 4)
+    def twin_grads(k):
         main, tail = tower_weight_grad(k * 2 + 1 - core)
         w_pair_out[k, :depth, :] = main.astype(BF16)
         w_pair_out[k, depth:, :] = tail.astype(BF16)
         remote(
             w_pair_out.at[k], w_pair_in.at[k], tp_send, tp_recv.at[k], seg, twin, dp
         ).start()
-        return carry
-
-    lax.fori_loop(0, 4, twin_grads, 0)
-
-    def send_piece(k, to, slot):
-        remote(
-            w_z_out.at[k], w_z_in.at[slot], tz_send.at[slot], tz_recv.at[slot], *to
-        ).start()
-
-    for k in (2, 1, 0, 3):
+
+    def own_grads(k):
         main, tail = tower_weight_grad(k * 2 + core)
         wait_bytes(w_pair_in.at[k], tp_recv.at[k])
         main = main + w_pair_in[k, :depth, :].astype(F32)
         tail = tail + w_pair_in[k, depth:, :].astype(F32)
         w_z_out[k, :depth, :] = main.astype(BF16)
         w_z_out[k, depth:, :] = tail.astype(BF16)
-        if k == 2:
+
+    def send_piece(k, to, slot):
+        remote(
+            w_z_out.at[k], w_z_in.at[slot], tz_send.at[slot], tz_recv.at[slot], *to
+        ).start()
+
+    def slope_to_grad(p, here):
+        grad_pre = grad_wide[here] * slope[p, here]
+        slope[p, here] = grad_pre
+        return grad_pre
+
+    for g in range(side):
+        for p in (4, 5):
+            slope_to_grad(p, slice(g * quarter, (g + 1) * quarter))
+
+    for j in range(side):
+        group = lax.rem(chip // side + (2, 1, 3, 0)[j], side)
+        here = pl.ds(pl.multiple_of(group * quarter, quarter), quarter)
+
+        def two(i, total, here=here):
+            p = jnp.where(i == 2, 6, 2 * i)
+            for q in range(2):
+                grad_pre = slope_to_grad(p + q, here)
+                total = total + mm(grad_pre, weights[p + q, :depth, :], NT)
+            return total
+
+        total = jnp.zeros((quarter, width), F32)
+        for p in (4, 5):
+            total = total + mm(slope[p, here], weights[p, :depth, :], NT)
+        total = lax.fori_loop(0, 3, two, total)
+        d_out[pl.ds(group * side, side)] = total.astype(BF16).reshape(side, rows_here, width)
+
+        def send_grads(i, inner, group=group):
+            to = group * side + i
+
+            @pl.when(to != chip)
+            def _():
+                remote(
+                    d_out.at[to], d_in.at[chip], d_send, d_recv, seg, to * 2 + core, dp
+                ).start()
+
+            return inner
+
+        lax.fori_loop(0, side, send_grads, 0)
+        if j == 0:
+            twin_grads(2)
+        if j == 1:
+            own_grads(2)
             send_piece(2, (1 - seg, me, dp), 2)
+    d_in[chip] = d_out[chip]
+    for k in (1, 3, 0):
+        twin_grads(k)
+    for k in (1, 3, 0):
+        own_grads(k)
 
     wait_bytes(d_in.at[pl.ds(0, chips - 1)], d_recv)
     total = d_in[0].astype(F32)
@@ -597,9 +626,10 @@
     for k in (1, 3):
         wait_bytes(w_z_in.at[k], tz_recv.at[k])
         tower_sum = tower_sum + w_z_in[k].astype(F32)
+    turned_sum = tower_sum[:width].T
     for t in range(towers):
         here = slice(t * per_tower, (t + 1) * per_tower)
-        out_tower[t] = tower_sum[:width, here].astype(BF16)
+        out_tower[t] = turned_sum[here].astype(BF16)
         sum_row[t : t + 1, :] = tower_sum[width : width + 1, here]
     out_tower_row[...] = sum_row[0:towers, :].astype(BF16)
     wait_bytes(gain_b_in.at[pl.ds(0, chips - 1)], gb_recv)
@@ -616,8 +646,11 @@
     wait_bytes(d_in.at[pl.ds(0, chips - 1)], d_send)
     wait_bytes(g_in.at[pl.ds(0, 4 * count - 1)], g_send)
     for k in range(1, 4):
-        wait_bytes(own_piece, wz_send.at[k])
         wait_bytes(own_piece, tz_send.at[k])
+    for sem, part in halves:
+        wait_bytes(own_piece.at[part], wz_send.at[sem])
+    wait_bytes(own_piece, wz_send.at[1])
+    wait_bytes(own_piece, wz_send.at[2])
     for k in range(4):
         wait_bytes(own_piece, wp_send.at[k])
     wait_bytes(w_pair_in, tp_send)
@@ -629,7 +662,7 @@
     feats, routes, arms, targets, gain, w_gate, w_up, w_down, tower_in, tower_out = args
     batches, rows_here, width = feats.shape
     hidden_here = w_gate.shape[2]
-    cols = 8 * tower_in.shape[2]
+    cols = 8 * tower_in.shape[1]
     piece = jax.ShapeDtypeStruct((width + 16, cols), BF16)
     chips = count // 2
     blocks = 4 * count
@@ -641,7 +674,7 @@
         v((8, 2 * rows_here), F32),
         v(piece.shape, BF16),
         v((16, cols), F32),
-        v((8, tower_in.shape[2]), F32),
+        v((8, tower_in.shape[1]), F32),
         v((all_rows, cols), BF16),
         v((batches, rows_here, count * capacity), BF16),
         v((batches, count, capacity, width), BF16),
@@ -745,16 +778,17 @@
         count,
         capacity,
         features,
-        routes,
+        routes.transpose(0, 2, 1),
         arm_ids,
         targets,
         trunk_gain.reshape(1, width),
         gate_weight,
         up_weight,
         down_weight,
-        tower_in,
+        tower_in.transpose(0, 2, 1),
         tower_out,
     )
+    grads[3] = grads[3].transpose(0, 2, 1)
     return (*grads, grad_gain.reshape(width))
 
 

time: 162 us -> 154 us (0.951)
  local copies, waits for them, and re-layouts: 11.4 us -> 7.29 us
  Pallas kernels: 150 us -> 146 us
    unnamed x18 -> x16, local copies, waits for them, and re-layouts: 11.4 us -> 7.29 us
    pallas_call x1, Pallas kernels: 150 us -> 146 us  [run_step(): pl.pallas_call(functools.partial(step_kernel, loss_scale), out_shape=out_...]
where the time goes in v4:
time: 154 us
  Pallas kernels  146 us (95%)
  local copies, waits for them, and re-layouts  7.29 us (5%)
    pallas_call x1, Pallas kernels, run_step(): pl.pallas_call(functools.partial(step_kernel, loss_scale), out_shape=out_...  146 us
    unnamed x16, local copies, waits for them, and re-layouts  7.29 us

profile of v4, /device:TPU:1, one launch (start us, length us, event | category | flops | bytes accessed | tf_op | source)
XLA Modules:
  0.0 154.1 jit_solution(15706352492448400592)
XLA Ops:
  0.6 146.1 %shard_map.145 = (bf16[1,512,1024]{2,1,0:T(8,128)(2,1)}, bf16[1,512,1024]{2,1,0:T(8,128)(2,1)}, bf16[1,1024,512]{2,1,0:T(8,128)(2,1)}, bf16[7,64,512]{2,1,0:T(8,...) custom-call(bf16[2,64,512]{2,1,0:T(8,128)(2,1)} %feats.1, s32[2,2,64]{2,1,0:T(2,128)} %bitcast.7, s32[2,64]{1,0:T(2,128)} %arms.1, ...), custom_call_target="tpu_custom_call" | custom-call | tf_op jit(solution)/shard_map/pallas_call | solution.py:748
  146.8 0.0 copy-start.1
  146.8 2.4 %copy.22 = bf16[1,512,1024]{2,1,0:T(8,128)(2,1)} copy(bf16[1,512,1024]{2,1,0:T(8,128)(2,1)} %get-tuple-element.24) | data formatting | bytes 2097152
  149.1 0.0 copy-done.1
  149.1 0.0 copy-start
  149.1 1.0 copy.23
  150.1 0.6 copy-done
  150.7 0.0 copy-start.2
  150.7 1.0 copy.24
  151.7 0.4 copy-done.2
  152.0 0.0 copy-start.4
  152.0 0.8 copy.25
  152.8 0.0 copy-done.4
  152.8 0.0 copy-start.3
  152.8 0.6 copy.26
  153.4 0.1 copy-done.3
  153.5 0.6 copy.27
Async XLA Ops:
  146.8 2.4 %copy-start.1 = (bf16[1,512,1024]{2,1,0:T(8,128)(2,1)S(1)}, bf16[1,512,1024]{2,1,0:T(8,128)(2,1)}, u32[]{:S(2)}) copy-start(bf16[1,512,1024]{2,1,0:T(8,128)(2,1)} %get-tuple-element.25) | copy-start | bytes 3145732
  149.1 1.6 %copy-start = (bf16[1,1024,512]{2,1,0:T(8,128)(2,1)S(1)}, bf16[1,1024,512]{2,1,0:T(8,128)(2,1)}, u32[]{:S(2)}) copy-start(bf16[1,1024,512]{2,1,0:T(8,128)(2,1)} %get-tuple-element.26) | copy-start | bytes 3145732
  150.7 1.3 copy-start.2
  152.0 0.8 copy-start.4
  152.8 0.7 copy-start.3

commit v5 on v4

--- a/solution.py
+++ b/solution.py
@@ -343,7 +343,6 @@
 
     lax.fori_loop(0, 4, turn, 0)
 
-    relay_half(*halves[0])
     wait_bytes(r_in, p_recv)
     own_table = tables[seg]
     added = mm(own_table, wide(r_in[pl.ds(0, count)]))
@@ -351,16 +350,16 @@
         added = added + mm(own_table, wide(r_in[pl.ds(z * count, count)]))
     mixed[chip] = (feats[seg].astype(F32) + added).astype(BF16)
 
-    def send_rows(i, carry):
-        to = lax.rem(chip + i, chips)
-        block = mixed.at[chip]
-        remote(block, block, m_send, m_recv.at[chip // side], seg, to * 2 + core, dp).start()
-        return carry
-
-    lax.fori_loop(1, chips, send_rows, 0)
-    relay_half(*halves[1])
-    far = weights.at[6 + core]
-    remote(far, far, wp_send.at[3], wp_recv.at[3], seg, twin, dp).start()
+    across, along = chip // side, lax.rem(chip, side)
+    for ahead in (0, 1, 3, 2):
+
+        def send_rows(i, carry, ahead=ahead):
+            to = lax.rem(across + ahead, side) * side + lax.rem(along + i, side)
+            block = mixed.at[chip]
+            remote(block, block, m_send, m_recv.at[across], seg, to * 2 + core, dp).start()
+            return carry
+
+        lax.fori_loop(0 if ahead else 1, side, send_rows, 0)
 
     depth = width
     out_cols = own_piece.shape[1]
@@ -390,8 +389,8 @@
             values[:, here] += part
 
     wait_bytes(weights.at[0], wp_recv.at[0])
-    for j, ahead in enumerate((0, 1, 3, 2)):
-        group = lax.rem(chip // side + ahead, side)
+    for j, ahead in enumerate((0, 3, 1, 2)):
+        group = lax.rem(across + ahead, side)
         if ahead == 0:
             wait_bytes(mixed.at[pl.ds(0, side - 1)], m_recv.at[group])
         else:
@@ -405,6 +404,12 @@
             return carry
 
         lax.fori_loop(1, 4, more, 0)
+        if j == 0:
+            relay_half(*halves[0])
+        if j == 1:
+            relay_half(*halves[1])
+            far = weights.at[6 + core]
+            remote(far, far, wp_send.at[3], wp_recv.at[3], seg, twin, dp).start()
     for k in (3, 2):
         if k == 2:
             relay_weights(2)
@@ -478,10 +483,18 @@
         w_z_out[k, :depth, :] = main.astype(BF16)
         w_z_out[k, depth:, :] = tail.astype(BF16)
 
-    def send_piece(k, to, slot):
+    inner, outer = (1 - seg, me, dp), (1 - seg, me, 1 - dp)
+    upper, lower_part = halves[0][1], halves[1][1]
+
+    def send_piece(k, part, to, sem):
         remote(
-            w_z_out.at[k], w_z_in.at[slot], tz_send.at[slot], tz_recv.at[slot], *to
+            w_z_out.at[k, part], w_z_in.at[k, part], tz_send.at[sem], tz_recv.at[sem], *to
         ).start()
+
+    def add_passing(k, part, sem):
+        passing = w_z_in.at[2, part]
+        wait_bytes(passing, tz_recv.at[sem])
+        w_z_out[k, part] = (w_z_out[k, part].astype(F32) + passing[...].astype(F32)).astype(BF16)
 
     def slope_to_grad(p, here):
         grad_pre = grad_wide[here] * slope[p, here]
@@ -525,12 +538,17 @@
             twin_grads(2)
         if j == 1:
             own_grads(2)
-            send_piece(2, (1 - seg, me, dp), 2)
+            send_piece(2, upper, inner, 0)
+            send_piece(2, lower_part, outer, 1)
     d_in[chip] = d_out[chip]
-    for k in (1, 3, 0):
-        twin_grads(k)
-    for k in (1, 3, 0):
-        own_grads(k)
+    twin_grads(1)
+    twin_grads(3)
+    own_grads(1)
+    send_piece(1, upper, inner, 2)
+    own_grads(3)
+    send_piece(3, lower_part, outer, 5)
+    twin_grads(0)
+    own_grads(0)
 
     wait_bytes(d_in.at[pl.ds(0, chips - 1)], d_recv)
     total = d_in[0].astype(F32)
@@ -549,10 +567,10 @@
     lax.fori_loop(1, 4 * count, spread, 0)
     pltpu.make_async_copy(b_out.at[me], g_in.at[z_mine * count + me], g_recv.at[z_mine]).start()
 
-    send_piece(1, (1 - seg, me, dp), 1)
-    wait_bytes(w_z_in.at[2], tz_recv.at[2])
-    w_z_out[3] = (w_z_out[3].astype(F32) + w_z_in[2].astype(F32)).astype(BF16)
-    send_piece(3, (1 - seg, me, 1 - dp), 3)
+    add_passing(3, upper, 0)
+    send_piece(3, upper, outer, 4)
+    add_passing(1, lower_part, 1)
+    send_piece(1, lower_part, inner, 3)
 
     def backward(j, carry):
         z = lax.rem(z_mine + j, 4)
@@ -623,8 +641,14 @@
     lax.fori_loop(half, hidden_here // strip, down_grads, 0)
 
     tower_sum = w_z_out[0].astype(F32)
+    for k, part, sem in (
+        (1, upper, 2),
+        (1, lower_part, 3),
+        (3, upper, 4),
+        (3, lower_part, 5),
+    ):
+        wait_bytes(w_z_in.at[k, part], tz_recv.at[sem])
     for k in (1, 3):
-        wait_bytes(w_z_in.at[k], tz_recv.at[k])
         tower_sum = tower_sum + w_z_in[k].astype(F32)
     turned_sum = tower_sum[:width].T
     for t in range(towers):
@@ -645,8 +669,8 @@
     wait_bytes(value_in.at[pl.ds(0, chips - 1)], v_send)
     wait_bytes(d_in.at[pl.ds(0, chips - 1)], d_send)
     wait_bytes(g_in.at[pl.ds(0, 4 * count - 1)], g_send)
-    for k in range(1, 4):
-        wait_bytes(own_piece, tz_send.at[k])
+    for sem, part in enumerate((upper, lower_part, upper, lower_part, upper, lower_part)):
+        wait_bytes(own_piece.at[part], tz_send.at[sem])
     for sem, part in halves:
         wait_bytes(own_piece.at[part], wz_send.at[sem])
     wait_bytes(own_piece, wz_send.at[1])
@@ -729,8 +753,8 @@
         dma((4,)),
         dma(()),
         dma((4,)),
-        dma((4,)),
-        dma((4,)),
+        dma((6,)),
+        dma((6,)),
         dma(()),
         dma(()),
         dma(()),

time: 154 us -> 148 us (0.961)
  Pallas kernels: 146 us -> 140 us
    pallas_call x1, Pallas kernels: 146 us -> 140 us  [run_step(): pl.pallas_call(functools.partial(step_kernel, loss_scale), out_shape=out_...]
where the time goes in v5:
time: 148 us
  Pallas kernels  140 us (95%)
  local copies, waits for them, and re-layouts  7.29 us (5%)
    pallas_call x1, Pallas kernels, run_step(): pl.pallas_call(functools.partial(step_kernel, loss_scale), out_shape=out_...  140 us
    unnamed x16, local copies, waits for them, and re-layouts  7.29 us

profile of v5, /device:TPU:1, one launch (start us, length us, event | category | flops | bytes accessed | tf_op | source)
XLA Modules:
  0.0 147.9 jit_solution(15161228258675137450)
XLA Ops:
  0.6 139.9 %shard_map.145 = (bf16[1,512,1024]{2,1,0:T(8,128)(2,1)}, bf16[1,512,1024]{2,1,0:T(8,128)(2,1)}, bf16[1,1024,512]{2,1,0:T(8,128)(2,1)}, bf16[7,64,512]{2,1,0:T(8,...) custom-call(bf16[2,64,512]{2,1,0:T(8,128)(2,1)} %feats.1, s32[2,2,64]{2,1,0:T(2,128)} %bitcast.7, s32[2,64]{1,0:T(2,128)} %arms.1, ...), custom_call_target="tpu_custom_call" | custom-call | tf_op jit(solution)/shard_map/pallas_call | solution.py:772
  140.6 0.0 copy-start.1
  140.6 2.4 %copy.22 = bf16[1,512,1024]{2,1,0:T(8,128)(2,1)} copy(bf16[1,512,1024]{2,1,0:T(8,128)(2,1)} %get-tuple-element.24) | data formatting | bytes 2097152
  142.9 0.0 copy-done.1
  143.0 0.0 copy-start
  143.0 1.0 copy.23
  143.9 0.6 copy-done
  144.6 0.0 copy-start.2
  144.6 1.0 copy.24
  145.5 0.4 copy-done.2
  145.9 0.0 copy-start.4
  145.9 0.8 copy.25
  146.7 0.0 copy-done.4
  146.7 0.0 copy-start.3
  146.7 0.6 copy.26
  147.2 0.1 copy-done.3
  147.3 0.6 copy.27
Async XLA Ops:
  140.6 2.4 %copy-start.1 = (bf16[1,512,1024]{2,1,0:T(8,128)(2,1)S(1)}, bf16[1,512,1024]{2,1,0:T(8,128)(2,1)}, u32[]{:S(2)}) copy-start(bf16[1,512,1024]{2,1,0:T(8,128)(2,1)} %get-tuple-element.25) | copy-start | bytes 3145732
  143.0 1.6 %copy-start = (bf16[1,1024,512]{2,1,0:T(8,128)(2,1)S(1)}, bf16[1,1024,512]{2,1,0:T(8,128)(2,1)}, u32[]{:S(2)}) copy-start(bf16[1,1024,512]{2,1,0:T(8,128)(2,1)} %get-tuple-element.26) | copy-start | bytes 3145732
  144.6 1.3 copy-start.2
  145.9 0.8 copy-start.4
  146.7 0.7 copy-start.3

commit v6 on v5

--- a/solution.py
+++ b/solution.py
@@ -547,8 +547,6 @@
     send_piece(1, upper, inner, 2)
     own_grads(3)
     send_piece(3, lower_part, outer, 5)
-    twin_grads(0)
-    own_grads(0)
 
     wait_bytes(d_in.at[pl.ds(0, chips - 1)], d_recv)
     total = d_in[0].astype(F32)
@@ -571,6 +569,8 @@
     send_piece(3, upper, outer, 4)
     add_passing(1, lower_part, 1)
     send_piece(1, lower_part, inner, 3)
+    twin_grads(0)
+    own_grads(0)
 
     def backward(j, carry):
         z = lax.rem(z_mine + j, 4)

time: 148 us -> 148 us (level)
  no operation moved by 1% of the time
where the time goes in v6:
time: 148 us
  Pallas kernels  140 us (95%)
  local copies, waits for them, and re-layouts  7.29 us (5%)
    pallas_call x1, Pallas kernels, run_step(): pl.pallas_call(functools.partial(step_kernel, loss_scale), out_shape=out_...  140 us
    unnamed x16, local copies, waits for them, and re-layouts  7.29 us

profile of v6, /device:TPU:1, one launch (start us, length us, event | category | flops | bytes accessed | tf_op | source)
XLA Modules:
  0.0 147.9 jit_solution(15266676646020129531)
XLA Ops:
  0.6 139.9 %shard_map.145 = (bf16[1,512,1024]{2,1,0:T(8,128)(2,1)}, bf16[1,512,1024]{2,1,0:T(8,128)(2,1)}, bf16[1,1024,512]{2,1,0:T(8,128)(2,1)}, bf16[7,64,512]{2,1,0:T(8,...) custom-call(bf16[2,64,512]{2,1,0:T(8,128)(2,1)} %feats.1, s32[2,2,64]{2,1,0:T(2,128)} %bitcast.7, s32[2,64]{1,0:T(2,128)} %arms.1, ...), custom_call_target="tpu_custom_call" | custom-call | tf_op jit(solution)/shard_map/pallas_call | solution.py:772
  140.6 0.0 copy-start.1
  140.6 2.4 %copy.22 = bf16[1,512,1024]{2,1,0:T(8,128)(2,1)} copy(bf16[1,512,1024]{2,1,0:T(8,128)(2,1)} %get-tuple-element.24) | data formatting | bytes 2097152
  142.9 0.0 copy-done.1
  142.9 0.0 copy-start
  142.9 1.0 copy.23
  143.9 0.6 copy-done
  144.5 0.0 copy-start.2
  144.5 1.0 copy.24
  145.5 0.4 copy-done.2
  145.9 0.0 copy-start.4
  145.9 0.8 copy.25
  146.6 0.0 copy-done.4
  146.6 0.0 copy-start.3
  146.6 0.6 copy.26
  147.2 0.1 copy-done.3
  147.3 0.6 copy.27
Async XLA Ops:
  140.6 2.4 %copy-start.1 = (bf16[1,512,1024]{2,1,0:T(8,128)(2,1)S(1)}, bf16[1,512,1024]{2,1,0:T(8,128)(2,1)}, u32[]{:S(2)}) copy-start(bf16[1,512,1024]{2,1,0:T(8,128)(2,1)} %get-tuple-element.25) | copy-start | bytes 3145732
  142.9 1.6 %copy-start = (bf16[1,1024,512]{2,1,0:T(8,128)(2,1)S(1)}, bf16[1,1024,512]{2,1,0:T(8,128)(2,1)}, u32[]{:S(2)}) copy-start(bf16[1,1024,512]{2,1,0:T(8,128)(2,1)} %get-tuple-element.26) | copy-start | bytes 3145732
  144.5 1.3 copy-start.2
  145.9 0.8 copy-start.4
  146.6 0.7 copy-start.3
